TPU v7x, 32 devices: a whole 2x2x4 slice. The times are simulated.
32 devices in a mesh: grp: 4 (over y, x), rep: 8 (over z, core).
Axes of the slice: x: 2, y: 2, z: 4, core: 2. Of those that a mesh axis runs over, the one named last changes fastest.
Arguments:
- inputs: bfloat16 [8, 512, 768], P('rep', 'grp'), may hold values from -6 to 6
- qkv_weight: bfloat16 [768, 2304], P('grp'), may hold values from -0.21650635 to 0.21650635
- qkv_bias: bfloat16 [2304], P('grp'), may hold values from -3 to 3
- out_weight: bfloat16 [768, 768], P('grp'), may hold values from -0.625 to 0.625
- out_bias: bfloat16 [768], P('grp'), may hold values from -3 to 3
- up_weight: bfloat16 [768, 3072], P('grp'), may hold values from -0.21875 to 0.21875
- up_bias: bfloat16 [3072], P('grp'), may hold values from -3 to 3
- down_weight: bfloat16 [3072, 768], P('grp'), may hold values from -0.109375 to 0.109375
- down_bias: bfloat16 [768], P('grp'), may hold values from -3 to 3
- attn_gain: bfloat16 [768], P('grp'), may hold values from 0.5 to 1.5
- attn_shift: bfloat16 [768], P('grp'), may hold values from -2 to 2
- mlp_gain: bfloat16 [768], P('grp'), may hold values from 0.5 to 1.5
- mlp_shift: bfloat16 [768], P('grp'), may hold values from -2 to 2
- cotangent: float32 [8, 512, 768], P('rep', 'grp'), may hold values from -6 to 6
Outputs:
- block_out: float32 [8, 512, 768], P('rep', 'grp')
- input_grad: float32 [8, 512, 768], P('rep', 'grp')
- qkv_weight_grad: float32 [768, 2304], P('grp')
- qkv_bias_grad: float32 [2304], P('grp')
- out_weight_grad: float32 [768, 768], P('grp')
- out_bias_grad: float32 [768], P('grp')
- up_weight_grad: float32 [768, 3072], P('grp')
- up_bias_grad: float32 [3072], P('grp')
- down_weight_grad: float32 [3072, 768], P('grp')
- down_bias_grad: float32 [768], P('grp')
- attn_gain_grad: float32 [768], P('grp')
- attn_shift_grad: float32 [768], P('grp')
- mlp_gain_grad: float32 [768], P('grp')
- mlp_shift_grad: float32 [768], P('grp')
All inputs are finite; a program needn't handle non-finite values.
Results may differ from a plain program's by a relative error of at most 0.0093.
Values may be sent and summed in bfloat16 or wider, within the bound.
A program may use at most 128 MiB of HBM per device.

v0:
```python
import jax
import jax.numpy as jnp
from jax import lax
from jax.sharding import PartitionSpec as P

D = 768
HEADS = 12
HD = 64
ROT = 16


eps = 1e-05


def layer_norm(values):
    centered = values - jnp.mean(values, axis=-1, keepdims=True)
    variance = jnp.mean(centered * centered, axis=-1, keepdims=True)
    inverse = lax.rsqrt(variance + eps)
    return (centered * inverse, inverse)


def gelu_parts(preact):
    normal_cdf = 0.5 * (1.0 + jax.scipy.special.erf(preact * 0.7071067811865476))
    density = jnp.exp(-0.5 * preact * preact) * 0.3989422804014327
    return (preact * normal_cdf, normal_cdf + preact * density)


def angle_tables(positions):
    half_rot = ROT // 2
    frequency = 10000.0 ** (-jnp.arange(half_rot, dtype=jnp.float32) * (2.0 / ROT))
    angles = positions.astype(jnp.float32)[:, None] * frequency[None, :]
    return (jnp.cos(angles)[:, None, :], jnp.sin(angles)[:, None, :])


def rotate(tensor, cos_table, sin_table):
    half_rot = ROT // 2
    lower_part = tensor[..., :half_rot]
    upper_part = tensor[..., half_rot:ROT]
    return jnp.concatenate(
        [
            lower_part * cos_table - upper_part * sin_table,
            upper_part * cos_table + lower_part * sin_table,
            tensor[..., ROT:],
        ],
        axis=-1,
    )


def unrotate(tensor, cos_table, sin_table):
    half_rot = ROT // 2
    lower_part = tensor[..., :half_rot]
    upper_part = tensor[..., half_rot:ROT]
    return jnp.concatenate(
        [
            lower_part * cos_table + upper_part * sin_table,
            upper_part * cos_table - lower_part * sin_table,
            tensor[..., ROT:],
        ],
        axis=-1,
    )


def local(
    inputs,
    qkv_weight,
    qkv_bias,
    out_weight,
    out_bias,
    up_weight,
    up_bias,
    down_weight,
    down_bias,
    attn_gain,
    attn_shift,
    mlp_gain,
    mlp_shift,
    cotangent,
):
    tokens = inputs.shape[1]
    (
        full_qkv,
        full_qkv_bias,
        full_out,
        full_out_bias,
        full_up,
        full_up_bias,
        full_down,
        full_down_bias,
        gain_attn,
        shift_attn,
        gain_mlp,
        shift_mlp,
    ) = (
        lax.all_gather(qkv_weight, "grp", axis=0, tiled=True),
        lax.all_gather(qkv_bias, "grp", axis=0, tiled=True),
        lax.all_gather(out_weight, "grp", axis=0, tiled=True),
        lax.all_gather(out_bias, "grp", axis=0, tiled=True),
        lax.all_gather(up_weight, "grp", axis=0, tiled=True),
        lax.all_gather(up_bias, "grp", axis=0, tiled=True),
        lax.all_gather(down_weight, "grp", axis=0, tiled=True),
        lax.all_gather(down_bias, "grp", axis=0, tiled=True),
        lax.all_gather(attn_gain, "grp", axis=0, tiled=True),
        lax.all_gather(attn_shift, "grp", axis=0, tiled=True),
        lax.all_gather(mlp_gain, "grp", axis=0, tiled=True),
        lax.all_gather(mlp_shift, "grp", axis=0, tiled=True),
    )
    first_row = lax.axis_index("grp") * tokens
    positions = first_row + jnp.arange(tokens, dtype=jnp.int32)
    cos_table, sin_table = angle_tables(positions)
    score_scale = HD ** (-0.5)
    hidden_in = inputs[0].astype(jnp.float32)
    normed, inverse = layer_norm(hidden_in)
    attn_in = (normed * gain_attn.astype(jnp.float32) + shift_attn.astype(jnp.float32)).astype(
        jnp.bfloat16
    )
    mlp_in = (normed * gain_mlp.astype(jnp.float32) + shift_mlp.astype(jnp.float32)).astype(
        jnp.bfloat16
    )
    qkv = jnp.dot(attn_in, full_qkv, preferred_element_type=jnp.float32) + full_qkv_bias.astype(
        jnp.float32
    )
    query_b = rotate(qkv[:, :D].reshape(tokens, HEADS, HD), cos_table, sin_table).astype(
        jnp.bfloat16
    )
    keys_local = (
        rotate(qkv[:, D : 2 * D].reshape(tokens, HEADS, HD), cos_table, sin_table)
        .astype(jnp.bfloat16)
        .reshape(tokens, D)
    )
    values_local = qkv[:, 2 * D :].astype(jnp.bfloat16)
    keys_all, values_all = (
        lax.all_gather(keys_local, "grp", axis=0, tiled=True),
        lax.all_gather(values_local, "grp", axis=0, tiled=True),
    )
    length = keys_all.shape[0]
    visible = jnp.arange(length, dtype=jnp.int32)[None, :] <= positions[:, None]
    query_heads = jnp.transpose(query_b, (1, 0, 2))
    key_heads = jnp.transpose(keys_all.reshape(length, HEADS, HD), (1, 0, 2))
    value_heads = jnp.transpose(values_all.reshape(length, HEADS, HD), (1, 0, 2))

    def forward_head(operands):
        query_one, key_one, value_one = operands
        scores = jnp.dot(query_one, key_one.T, preferred_element_type=jnp.float32) * score_scale
        scores = jnp.where(visible, scores, -jnp.inf)
        row_max = jnp.max(scores, axis=-1, keepdims=True)
        log_total = row_max + jnp.log(jnp.sum(jnp.exp(scores - row_max), axis=-1, keepdims=True))
        probs_b = jnp.exp(scores - log_total).astype(jnp.bfloat16)
        context_one = jnp.dot(probs_b, value_one, preferred_element_type=jnp.float32).astype(
            jnp.bfloat16
        )
        return (context_one, log_total)

    context_heads, log_totals = lax.map(forward_head, (query_heads, key_heads, value_heads))
    context = jnp.transpose(context_heads, (1, 0, 2)).reshape(tokens, D)
    attn_out = jnp.dot(
        context, full_out, preferred_element_type=jnp.float32
    ) + full_out_bias.astype(jnp.float32)
    preact = jnp.dot(mlp_in, full_up, preferred_element_type=jnp.float32) + full_up_bias.astype(
        jnp.float32
    )
    activation, slope = gelu_parts(preact)
    act_b = activation.astype(jnp.bfloat16)
    mlp_out = jnp.dot(act_b, full_down, preferred_element_type=jnp.float32) + full_down_bias.astype(
        jnp.float32
    )
    block_out = hidden_in + attn_out + mlp_out
    back_qkv, back_out, back_up, back_down, back_gain_attn, back_gain_mlp = (
        lax.all_gather(qkv_weight, "grp", axis=0, tiled=True),
        lax.all_gather(out_weight, "grp", axis=0, tiled=True),
        lax.all_gather(up_weight, "grp", axis=0, tiled=True),
        lax.all_gather(down_weight, "grp", axis=0, tiled=True),
        lax.all_gather(attn_gain, "grp", axis=0, tiled=True),
        lax.all_gather(mlp_gain, "grp", axis=0, tiled=True),
    )
    grad_out = cotangent[0]
    grad_b = grad_out.astype(jnp.bfloat16)
    down_grad = jnp.dot(act_b.T, grad_b, preferred_element_type=jnp.float32)
    out_grad = jnp.dot(context.T, grad_b, preferred_element_type=jnp.float32)
    bias_sum = jnp.sum(grad_out, axis=0)
    preact_grad = jnp.dot(grad_b, back_down.T, preferred_element_type=jnp.float32) * slope
    up_bias_grad = jnp.sum(preact_grad, axis=0)
    preact_b = preact_grad.astype(jnp.bfloat16)
    up_grad = jnp.dot(mlp_in.T, preact_b, preferred_element_type=jnp.float32)
    mlp_in_grad = jnp.dot(preact_b, back_up.T, preferred_element_type=jnp.float32)
    context_grad = jnp.dot(grad_b, back_out.T, preferred_element_type=jnp.float32).astype(
        jnp.bfloat16
    )
    context_grad_heads = jnp.transpose(context_grad.reshape(tokens, HEADS, HD), (1, 0, 2))

    def backward_head(operands):
        query_one, key_one, value_one, grad_one, log_total = operands
        scores = jnp.dot(query_one, key_one.T, preferred_element_type=jnp.float32) * score_scale
        scores = jnp.where(visible, scores, -jnp.inf)
        attn_probs = jnp.exp(scores - log_total)
        probs_b = attn_probs.astype(jnp.bfloat16)
        prob_grad = jnp.dot(grad_one, value_one.T, preferred_element_type=jnp.float32)
        row_dot = jnp.sum(attn_probs * prob_grad, axis=-1, keepdims=True)
        score_grad = (attn_probs * (prob_grad - row_dot) * score_scale).astype(jnp.bfloat16)
        query_grad = jnp.dot(score_grad, key_one, preferred_element_type=jnp.float32)
        key_grad = jnp.dot(score_grad.T, query_one, preferred_element_type=jnp.float32)
        value_grad = jnp.dot(probs_b.T, grad_one, preferred_element_type=jnp.float32)
        return (query_grad, key_grad, value_grad)

    query_grads, key_grads, value_grads = lax.map(
        backward_head, (query_heads, key_heads, value_heads, context_grad_heads, log_totals)
    )
    key_full = jnp.transpose(key_grads, (1, 0, 2)).reshape(length, D)
    value_full = jnp.transpose(value_grads, (1, 0, 2)).reshape(length, D)
    key_mine, value_mine = (
        lax.psum_scatter(key_full, "grp", scatter_dimension=0, tiled=True),
        lax.psum_scatter(value_full, "grp", scatter_dimension=0, tiled=True),
    )
    query_rows = unrotate(jnp.transpose(query_grads, (1, 0, 2)), cos_table, sin_table).reshape(
        tokens, D
    )
    key_rows = unrotate(key_mine.reshape(tokens, HEADS, HD), cos_table, sin_table).reshape(
        tokens, D
    )
    qkv_rows = jnp.concatenate([query_rows, key_rows, value_mine], axis=1)
    qkv_bias_grad = jnp.sum(qkv_rows, axis=0)
    qkv_rows_b = qkv_rows.astype(jnp.bfloat16)
    qkv_grad = jnp.dot(attn_in.T, qkv_rows_b, preferred_element_type=jnp.float32)
    attn_in_grad = jnp.dot(qkv_rows_b, back_qkv.T, preferred_element_type=jnp.float32)
    attn_gain_grad = jnp.sum(attn_in_grad * normed, axis=0)
    attn_shift_grad = jnp.sum(attn_in_grad, axis=0)
    mlp_gain_grad = jnp.sum(mlp_in_grad * normed, axis=0)
    mlp_shift_grad = jnp.sum(mlp_in_grad, axis=0)
    normed_grad = attn_in_grad * back_gain_attn.astype(
        jnp.float32
    ) + mlp_in_grad * back_gain_mlp.astype(jnp.float32)
    input_grad = grad_out + inverse * (
        normed_grad
        - jnp.mean(normed_grad, axis=-1, keepdims=True)
        - normed * jnp.mean(normed_grad * normed, axis=-1, keepdims=True)
    )
    group_parts = (
        lax.psum_scatter(qkv_grad, "grp", scatter_dimension=0, tiled=True),
        lax.psum_scatter(qkv_bias_grad, "grp", scatter_dimension=0, tiled=True),
        lax.psum_scatter(out_grad, "grp", scatter_dimension=0, tiled=True),
        lax.psum_scatter(bias_sum, "grp", scatter_dimension=0, tiled=True),
        lax.psum_scatter(up_grad, "grp", scatter_dimension=0, tiled=True),
        lax.psum_scatter(up_bias_grad, "grp", scatter_dimension=0, tiled=True),
        lax.psum_scatter(down_grad, "grp", scatter_dimension=0, tiled=True),
        lax.psum_scatter(attn_gain_grad, "grp", scatter_dimension=0, tiled=True),
        lax.psum_scatter(attn_shift_grad, "grp", scatter_dimension=0, tiled=True),
        lax.psum_scatter(mlp_gain_grad, "grp", scatter_dimension=0, tiled=True),
        lax.psum_scatter(mlp_shift_grad, "grp", scatter_dimension=0, tiled=True),
    )
    (
        qkv_part,
        qkv_bias_part,
        out_part,
        bias_part,
        up_part,
        up_bias_part,
        down_part,
        gain_attn_part,
        shift_attn_part,
        gain_mlp_part,
        shift_mlp_part,
    ) = group_parts
    (
        qkv_total,
        qkv_bias_total,
        out_total,
        bias_total,
        up_total,
        up_bias_total,
        down_total,
        gain_attn_total,
        shift_attn_total,
        gain_mlp_total,
        shift_mlp_total,
    ) = lax.psum(
        (
            qkv_part,
            qkv_bias_part,
            out_part,
            bias_part,
            up_part,
            up_bias_part,
            down_part,
            gain_attn_part,
            shift_attn_part,
            gain_mlp_part,
            shift_mlp_part,
        ),
        "rep",
    )
    return (
        block_out[None],
        input_grad[None],
        qkv_total,
        qkv_bias_total,
        out_total,
        bias_total,
        up_total,
        up_bias_total,
        down_total,
        bias_total,
        gain_attn_total,
        shift_attn_total,
        gain_mlp_total,
        shift_mlp_total,
    )


def solution(mesh):
    placed = (
        P("rep", "grp", None),
        P("grp", None),
        P("grp"),
        P("grp", None),
        P("grp"),
        P("grp", None),
        P("grp"),
        P("grp", None),
        P("grp"),
        P("grp"),
        P("grp"),
        P("grp"),
        P("grp"),
        P("rep", "grp", None),
    )
    return jax.shard_map(
        local,
        mesh=mesh,
        in_specs=placed,
        out_specs=(
            P("rep", "grp", None),
            P("rep", "grp", None),
            P("grp", None),
            P("grp"),
            P("grp", None),
            P("grp"),
            P("grp", None),
            P("grp"),
            P("grp", None),
            P("grp"),
            P("grp"),
            P("grp"),
            P("grp"),
            P("grp"),
        ),
        check_vma=False,
    )
```

profile of v0, /device:TPU:0, one launch (start us, length us, event | category | flops | bytes accessed | tf_op | source)
XLA Modules:
  0.0 870.5 jit_solution(10710567366324979250)
XLA Ops:
  8.8 1.3 fusion.99
  17.3 18.7 %all-reduce.17 = (bf16[768]{0:T(1024)(128)(2,1)}, bf16[768]{0:T(1024)(128)(2,1)}, bf16[768]{0:T(1024)(128)(2,1)}, bf16[2304]{0:T(1024)(128)(2,1)S(1)}, bf16[768]...) all-reduce(bf16[768]{0:T(1024)(128)(2,1)S(1)} %dynamic-update-slice, ...), channel_id=1, replica_groups=mesh['grp'=4,'rep'=8] {'grp'}, use_global_device_ids=true, to_apply=%add.6 | all-reduce | flops 6912 | bytes 27648
  37.5 3.0 all-gather.8.cloned.1.call-done
  40.5 1.8 fusion.102
  43.2 46.4 %all-gather.6.cloned.1.call-done = bf16[768,2304]{1,0:T(8,128)(2,1)} async-done(((bf16[192,2304]{1,0:T(8,128)(2,1)}), bf16[768,2304]{1,0:T(8,128)(2,1)}) %all-gather.6.cloned.1.call-update) | async-done | bytes 3538960 | tf_op jit(solution)/shard_map/all_gather | solution.py:94
  89.5 2.7 convolution_add_fusion
  93.1 11.1 %all_gather.52 = bf16[512,768]{0,1:T(8,128)(2,1)S(1)} all-gather(bf16[128,768]{0,1:T(8,128)(2,1)S(1)} %bitcast.246), channel_id=1, replica_groups=mesh['grp'=4,'rep'=8] {'grp'}, dimensions={0}, use_global_device_ids=true | all-gather | bytes 983040 | tf_op jit(solution)/shard_map/all_gather | solution.py:132
  104.2 11.1 %all_gather.53 = bf16[512,768]{1,0:T(8,128)(2,1)S(1)} all-gather(bf16[128,768]{1,0:T(8,128)(2,1)S(1)} %slice.97), channel_id=1, replica_groups=mesh['grp'=4,'rep'=8] {'grp'}, dimensions={0}, use_global_device_ids=true | all-gather | bytes 983040 | tf_op jit(solution)/shard_map/all_gather | solution.py:133
  115.6 1.5 copy.55
  118.0 26.1 %while.28 = (s32[]{:T(128)}, bf16[12,128,64]{1,2,0:T(8,128)(2,1)S(1)}, f32[12,128,1]{1,2,0:T(1,128)}, bf16[12,128,64]{2,1,0:T(8,128)(2,1)S(1)}, bf16[12,512,64]{...) while((s32[]{:T(128)}, ...), condition=%wide.region_5.6_spmd.clone, body=%wide.region_2.5_spmd.clone.sunk | while | flops 17309568 | bytes 1104481 | solution.py:153
  144.1 58.0 %while.29 = (s32[]{:T(128)}, f32[12,128,64]{1,2,0:T(8,128)S(1)}, f32[12,512,64]{1,2,0:T(8,128)}, f32[12,512,64]{1,2,0:T(8,128)}, bf16[12,128,64]{2,1,0:T(8,128)(...) while((s32[]{:T(128)}, f32[12,128,64]{1,2,0:T(8,128)S(1)}, ...), condition=%wide.region_8.9_spmd.clone, body=%wide.region_6.8_spmd.clone.sunk | while | flops 42663808 | bytes 2760825 | solution.py:204
  146.6 1.5 fusion.159
  151.4 1.5 fusion.159
  156.2 1.5 fusion.159
  161.1 1.5 fusion.159
  165.9 1.5 fusion.159
  170.7 1.5 fusion.159
  175.6 1.5 fusion.159
  180.4 1.5 fusion.159
  185.3 1.5 fusion.159
  190.1 1.5 fusion.159
  194.9 1.5 fusion.159
  199.8 1.5 fusion.159
  204.0 1.9 fusion.78
  205.9 27.6 %reduce-scatter.7.cloned.1.call-done = f32[128,768]{0,1:T(8,128)} async-done(((f32[512,768]{0,1:T(8,128)}), f32[128,768]{0,1:T(8,128)}) %reduce-scatter.7.cloned.1.call-update) | async-done | bytes 393232 | tf_op jit(solution)/shard_map/reduce_scatter | solution.py:210
  235.5 32.1 %reduce-scatter.9.cloned.1.call-done = f32[128,768]{0,1:T(8,128)} async-done(((f32[512,768]{0,1:T(8,128)}), f32[128,768]{0,1:T(8,128)}) %reduce-scatter.9.cloned.1.call-update) | async-done | bytes 393232 | tf_op jit(solution)/shard_map/reduce_scatter | solution.py:211
  267.6 5.1 fusion.83
  273.4 8.3 all-gather
  281.7 44.5 %all-gather.10.cloned.1.call-done = bf16[768,3072]{1,0:T(8,128)(2,1)} async-done(((bf16[192,3072]{1,0:T(8,128)(2,1)}), bf16[768,3072]{1,0:T(8,128)(2,1)}) %all-gather.10.cloned.1.call-update) | async-done | bytes 4718608 | tf_op jit(solution)/shard_map/all_gather | solution.py:98
  326.2 3.2 convolution_add_fusion.1
  329.4 5.1 fusion.81
  334.7 50.2 %all-gather.12.cloned.1.call-done = bf16[3072,768]{1,0:T(8,128)(2,1)} async-done(((bf16[768,768]{1,0:T(8,128)(2,1)}), bf16[3072,768]{1,0:T(8,128)(2,1)}) %all-gather.12.cloned.1.call-update) | async-done | bytes 4718608 | tf_op jit(solution)/shard_map/all_gather | solution.py:100
  384.9 4.1 fusion.100
  389.9 5.2 fusion.74
  395.1 30.9 %reduce-scatter.13.cloned.1.call-done = f32[192,768]{1,0:T(8,128)} async-done(((f32[768,768]{1,0:T(8,128)}), f32[192,768]{1,0:T(8,128)}) %reduce-scatter.13.cloned.1.call-update) | async-done | bytes 589840 | tf_op jit(solution)/shard_map/reduce_scatter | solution.py:239
  425.9 79.6 %reduce-scatter.11.cloned.1.call-done = f32[192,2304]{1,0:T(8,128)} async-done(((f32[768,2304]{1,0:T(8,128)}), f32[192,2304]{1,0:T(8,128)}) %reduce-scatter.11.cloned.1.call-update) | async-done | bytes 1769488 | tf_op jit(solution)/shard_map/reduce_scatter | solution.py:237
  505.6 98.0 %reduce-scatter.17.cloned.1.call-done = f32[768,768]{1,0:T(8,128)} async-done(((f32[3072,768]{1,0:T(8,128)}), f32[768,768]{1,0:T(8,128)}) %reduce-scatter.17.cloned.1.call-update) | async-done | bytes 2359312 | tf_op jit(solution)/shard_map/reduce_scatter | solution.py:243
  603.6 97.9 %reduce-scatter.15.cloned.1.call-done = f32[192,3072]{1,0:T(8,128)} async-done(((f32[768,3072]{1,0:T(8,128)}), f32[192,3072]{1,0:T(8,128)}) %reduce-scatter.15.cloned.1.call-update) | async-done | bytes 2359312 | tf_op jit(solution)/shard_map/reduce_scatter | solution.py:241
  703.6 3.4 convolution_add_fusion.3
  707.0 2.7 fusion.50
  710.1 1.3 fusion.85
  711.5 1.8 fusion.91
  713.3 15.9 %all-reduce.16 = (f32[2304]{0:T(1024)S(1)}, f32[768]{0:T(1024)S(1)}, f32[3072]{0:T(1024)S(1)}, f32[768]{0:T(1024)S(1)}, f32[768]{0:T(1024)S(1)}, /*index=5*/f32[768]{0:T(1024)S(1)}, f32[768]{0:T(1024)S(1)}) all-reduce(f32[2304]{0:T(1024)S(1)} %fusion.51, f32[768]{0:T(1024)S(1)} %reduce_sum.122, ...), channel_id=5, replica_groups=mesh['grp'=4,'rep'=8] {'grp'}, use_global_device_ids=true, to_apply=%region_16.17.clone | all-reduce | flops 9216 | bytes 73728
  729.7 28.2 %all-reduce.14 = (f32[576]{0:T(1024)}, f32[192]{0:T(256)S(1)}, f32[768]{0:T(1024)}, f32[192]{0:T(256)}, f32[192]{0:T(256)}, /*index=5*/f32[192]{0:T(256)}, f32[192]{0:T(256)}) all-reduce(f32[576]{0:T(1024)S(1)} %dynamic-slice.8, f32[192]{0:T(256)S(1)} %dynamic-slice.10, ...), channel_id=1, replica_groups=mesh['grp'=4,'rep'=8] {'rep'}, use_global_device_ids=true, to_apply=%region_17.18 | all-reduce | flops 2304 | bytes 18432 | tf_op jit(solution)/shard_map/psum | solution.py:274
  758.9 96.8 %all-reduce.20.cloned.1.call-done = (f32[192,2304]{1,0:T(8,128)}, f32[192,768]{1,0:T(8,128)}, f32[192,3072]{1,0:T(8,128)}, f32[768,768]{1,0:T(8,128)}) async-done(((f32[192,2304]{1,0:T(8,128)}, f32[192,768]{1,0:T(8,128)}, f32[192,3072]{1,0:T(8,128)}, f32[768,768]{1,0:T(8,128)}), (f32[192,2304]{1,0:T(8,128)}, f32[192,768]{1,0:T(8,128)}, f32[192,3072]{1,0:T(8,128)}, ...) | async-done | bytes 7077904 | tf_op jit(solution)/shard_map/psum | solution.py:274
  856.3 2.9 copy.103
  860.0 1.4 copy.105
  862.6 1.4 copy.106
  (258 shorter events, 86.9 us)
Async XLA Ops:
  7.2 30.0 %copy-start = (bf16[1,128,768]{2,1,0:T(8,128)(2,1)S(1)}, bf16[1,128,768]{2,1,0:T(8,128)(2,1)}, u32[]{:S(2)}) copy-start(bf16[1,128,768]{2,1,0:T(8,128)(2,1)} %param.18) | copy-start | bytes 589828
  7.2 33.3 %copy-start.2 = (f32[1,128,768]{2,1,0:T(8,128)S(1)}, f32[1,128,768]{2,1,0:T(8,128)}, u32[]{:S(2)}) copy-start(f32[1,128,768]{2,1,0:T(8,128)} %param.31) | copy-start | bytes 1179652
  7.2 33.3 %all-gather.8.cloned.1.call-start = ((), (), s32[]{:S(2)}) async-start(), calls=%async_computation.7 | async-start | bytes 1474560 | tf_op jit(solution)/shard_map/all_gather | solution.py:96
  7.9 81.6 %all-gather.6.cloned.1.call-start = ((), (), s32[]{:S(2)}) async-start(), calls=%async_computation.6 | async-start | bytes 4423680 | tf_op jit(solution)/shard_map/all_gather | solution.py:94
  8.7 224.9 %reduce-scatter.7.cloned.1.call-start = ((), (), s32[]{:S(2)}) async-start(), calls=%async_computation.10 | async-start | bytes 1966080 | tf_op jit(solution)/shard_map/reduce_scatter | solution.py:210
  37.4 54.8 %copy-start.14 = (f32[128]{0:T(128)}, f32[128]{0:T(128)S(1)}, u32[]{:S(2)}) copy-start(f32[128]{0:T(128)S(1)} %add_rsqrt_fusion) | copy-start | bytes 1540
  37.5 55.2 %copy-start.10 = (f32[128,8]{0,1:T(8,128)}, f32[128,8]{0,1:T(8,128)S(1)}, u32[]{:S(2)}) copy-start(f32[128,8]{0,1:T(8,128)S(1)} %get-tuple-element.276) | copy-start | bytes 12292
  37.5 55.2 %copy-start.12 = (f32[128,8]{0,1:T(8,128)}, f32[128,8]{0,1:T(8,128)S(1)}, u32[]{:S(2)}) copy-start(f32[128,8]{0,1:T(8,128)S(1)} %get-tuple-element.277) | copy-start | bytes 12292
  118.0 26.1 %copy-start.9 = (f32[12,128,64]{1,2,0:T(8,128)S(1)}, f32[12,128,64]{1,2,0:T(8,128)}, u32[]{:S(2)}) copy-start(f32[12,128,64]{1,2,0:T(8,128)} %custom-call.2) | copy-start | bytes 1179652
  202.2 65.4 %reduce-scatter.9.cloned.1.call-start = ((), (), s32[]{:S(2)}) async-start(), calls=%async_computation.11 | async-start | bytes 1966080 | tf_op jit(solution)/shard_map/reduce_scatter | solution.py:211
  202.8 123.5 %all-gather.10.cloned.1.call-start = ((), (), s32[]{:S(2)}) async-start(), calls=%async_computation.8 | async-start | bytes 5898240 | tf_op jit(solution)/shard_map/all_gather | solution.py:98
  203.3 181.6 %all-gather.12.cloned.1.call-start = ((), (), s32[]{:S(2)}) async-start(), calls=%async_computation.9 | async-start | bytes 5898240 | tf_op jit(solution)/shard_map/all_gather | solution.py:100
  203.9 222.0 %reduce-scatter.13.cloned.1.call-start = ((), (), s32[]{:S(2)}) async-start(), calls=%async_computation.13 | async-start | bytes 2949120 | tf_op jit(solution)/shard_map/reduce_scatter | solution.py:239
  205.8 28.7 %copy-start.11 = (f32[128,8]{0,1:T(8,128)S(1)}, f32[128,8]{0,1:T(8,128)}, u32[]{:S(2)}) copy-start(f32[128,8]{0,1:T(8,128)} %copy-done.10) | copy-start | bytes 12292
  205.8 28.7 %copy-start.13 = (f32[128,8]{0,1:T(8,128)S(1)}, f32[128,8]{0,1:T(8,128)}, u32[]{:S(2)}) copy-start(f32[128,8]{0,1:T(8,128)} %copy-done.12) | copy-start | bytes 12292
  205.9 299.7 %reduce-scatter.11.cloned.1.call-start = ((), (), s32[]{:S(2)}) async-start(), calls=%async_computation.12 | async-start | bytes 8847360 | tf_op jit(solution)/shard_map/reduce_scatter | solution.py:237
  205.9 61.7 %copy-start.15 = (f32[128]{0:T(128)S(1)}, f32[128]{0:T(128)}, u32[]{:S(2)}) copy-start(f32[128]{0:T(128)} %copy-done.14) | copy-start | bytes 1540
  272.7 0.7 copy-start.20
  272.7 0.7 copy-start.19
  272.7 0.7 copy-start.18
  272.7 330.9 %reduce-scatter.17.cloned.1.call-start = ((), (), s32[]{:S(2)}) async-start(), calls=%async_computation.15 | async-start | bytes 11796480 | tf_op jit(solution)/shard_map/reduce_scatter | solution.py:243
  334.5 367.0 %reduce-scatter.15.cloned.1.call-start = ((), (), s32[]{:S(2)}) async-start(), calls=%async_computation.14 | async-start | bytes 11796480 | tf_op jit(solution)/shard_map/reduce_scatter | solution.py:241
  389.0 0.9 copy-start.4
  395.0 460.7 %all-reduce.20.cloned.1.call-start = ((), (), s32[]{:S(2)}) async-start(), calls=%async_computation.16 | async-start | bytes 14155776 | tf_op jit(solution)/shard_map/psum | solution.py:274
  701.5 2.0 copy-start.17
  701.5 2.0 copy-start.16
  703.6 6.6 copy-start.1
  703.6 7.9 slice-start
  707.0 2.8 copy-start.3
  707.0 4.4 slice-start.1
  710.1 1.3 copy-start.5
  757.9 101.3 %copy-start.21 = (f32[192]{0:T(256)}, f32[192]{0:T(256)S(1)}, u32[]{:S(2)}) copy-start(f32[192]{0:T(256)S(1)} %get-tuple-element.492) | copy-start | bytes 2308
  856.3 3.0 copy-start.8
  856.3 3.8 copy-start.7
  860.0 2.5 copy-start.6
Sparse Core Ops, SparseCore 0:
  9.8 30.6 all-gather.7
  42.4 47.1 all-gather.5
  202.3 31.2 reduce-scatter.6
  236.4 31.1 reduce-scatter.8
  269.3 56.9 all-gather.9
  327.9 56.9 all-gather.11
  388.5 37.3 reduce-scatter.12
  429.0 76.5 reduce-scatter.10
  508.7 94.8 reduce-scatter.16
  606.6 94.8 reduce-scatter.14
  704.2 151.4 all-reduce.19
where the time goes:
time: 873 us; the launch traced here: 870 us
  waiting for transfers between devices  610 us (70%)
  matrix products  104 us (12%)
  blocking collectives  93.3 us (11%)
  local copies, waits for them, and re-layouts  30.6 us (4%)
  between operations  17.7 us (2%)
  other arithmetic  13.8 us (2%)
    reduce_scatter x1, waiting for transfers between devices, local(): lax.psum_scatter(down_grad, 'grp', scatter_dimension=0, tiled=True)  98 us
    reduce_scatter x1, waiting for transfers between devices, local(): lax.psum_scatter(up_grad, 'grp', scatter_dimension=0, tiled=True)  97.9 us
    psum x1, waiting for transfers between devices, local(): lax.psum((qkv_part, qkv_bias_part, out_part, bias_part, up_part, up_bias_...  96.8 us
    reduce_scatter x1, waiting for transfers between devices, local(): lax.psum_scatter(qkv_grad, 'grp', scatter_dimension=0, tiled=True)  79.6 us
    all_gather x1, waiting for transfers between devices, local(): lax.all_gather(down_weight, 'grp', axis=0, tiled=True)  50.2 us
    all_gather x1, waiting for transfers between devices, local(): lax.all_gather(qkv_weight, 'grp', axis=0, tiled=True)  46.4 us
    all_gather x1, waiting for transfers between devices, local(): lax.all_gather(up_weight, 'grp', axis=0, tiled=True)  44.5 us
    unnamed x2, blocking collectives  34.6 us
  transfers between devices with their start and end apart: 11, of which 11 were waited for; matrix products, arithmetic and copies ran while one was open for 6% of the time, Pallas kernels for 0%

commit v1 on v0

--- a/solution.py
+++ b/solution.py
@@ -60,7 +60,7 @@
     )
 
 
-def local(
+def local_by_tokens(
     inputs,
     qkv_weight,
     qkv_bias,
@@ -305,7 +305,211 @@
     )
 
 
+def rotary_tables(length):
+    half_rot = ROT // 2
+    frequency = 10000.0 ** (-jnp.arange(half_rot, dtype=jnp.float32) * (2.0 / ROT))
+    angles = jnp.arange(length, dtype=jnp.float32)[:, None] * frequency[None, :]
+    return (jnp.cos(angles)[:, None, :], jnp.sin(angles)[:, None, :])
+
+
+def gather(array):
+    return lax.all_gather(array, "grp", axis=0, tiled=True)
+
+
+def local_by_heads(
+    inputs,
+    qkv_weight,
+    qkv_bias,
+    out_weight,
+    out_bias,
+    up_weight,
+    up_bias,
+    down_weight,
+    down_bias,
+    attn_gain,
+    attn_shift,
+    mlp_gain,
+    mlp_shift,
+    cotangent,
+):
+    f32, bf16 = jnp.float32, jnp.bfloat16
+    group = lax.axis_size("grp")
+    me = lax.axis_index("grp")
+    tokens = inputs.shape[1]
+    length = group * tokens
+    rows = D // group
+    heads = HEADS // group
+    width = heads * HD
+    hidden = up_weight.shape[1] // group
+
+    def dot(a, b):
+        return jnp.dot(a, b, preferred_element_type=f32)
+
+    grad_out = cotangent[0]
+    x_all, grad_b = (gather(inputs[0]), gather(grad_out.astype(bf16)))
+    qkv_parts = jnp.transpose(qkv_weight.reshape(rows, 3, group, width), (2, 0, 1, 3)).reshape(
+        group, rows, 3 * width
+    )
+    up_parts = jnp.transpose(up_weight.reshape(rows, group, hidden), (1, 0, 2))
+    w_in = lax.all_to_all(
+        jnp.concatenate([qkv_parts, up_parts], axis=2), "grp", 0, 0, tiled=True
+    ).reshape(D, 3 * width + hidden)
+    w_qkv, w_up = w_in[:, : 3 * width], w_in[:, 3 * width :]
+    small = gather(
+        jnp.concatenate(
+            [qkv_bias, out_bias, down_bias, attn_gain, attn_shift, mlp_gain, mlp_shift]
+        )[None]
+    ).astype(f32)
+    nb = qkv_bias.shape[0]
+    bias_qkv = small[:, :nb].reshape(3, group, width)
+    bias_qkv = lax.dynamic_index_in_dim(bias_qkv, me, 1, keepdims=False).reshape(3 * width)
+    vec = [small[:, nb + i * rows : nb + (i + 1) * rows].reshape(D) for i in range(6)]
+    bias_out, bias_down, gain_attn, shift_attn, gain_mlp, shift_mlp = vec
+
+    hidden_in = x_all.astype(f32)
+    normed, inverse = layer_norm(hidden_in)
+    attn_in = (normed * gain_attn + shift_attn).astype(bf16)
+    mlp_in = (normed * gain_mlp + shift_mlp).astype(bf16)
+    qkv = dot(attn_in, w_qkv) + bias_qkv
+    cos_table, sin_table = rotary_tables(length)
+
+    def split(t):
+        return t.reshape(length, heads, HD)
+
+    query = jnp.transpose(
+        rotate(split(qkv[:, :width]), cos_table, sin_table).astype(bf16), (1, 0, 2)
+    )
+    keys = jnp.transpose(
+        rotate(split(qkv[:, width : 2 * width]), cos_table, sin_table).astype(bf16), (1, 0, 2)
+    )
+    values = jnp.transpose(split(qkv[:, 2 * width :]).astype(bf16), (1, 0, 2))
+    visible = (
+        jnp.arange(length, dtype=jnp.int32)[None, :] <= jnp.arange(length, dtype=jnp.int32)[:, None]
+    )
+    scale = HD ** (-0.5)
+
+    def bdot(eq, a, b):
+        return jnp.einsum(eq, a, b, preferred_element_type=f32)
+
+    scores = bdot("hqd,hkd->hqk", query, keys) * scale
+    scores = jnp.where(visible[None], scores, -jnp.inf)
+    row_max = jnp.max(scores, axis=-1, keepdims=True)
+    log_total = row_max + jnp.log(jnp.sum(jnp.exp(scores - row_max), axis=-1, keepdims=True))
+    attn_probs = jnp.exp(scores - log_total)
+    probs_b = attn_probs.astype(bf16)
+    context = jnp.transpose(bdot("hqk,hkd->qhd", probs_b, values).astype(bf16), (0, 1, 2)).reshape(
+        length, width
+    )
+    preact = dot(mlp_in, w_up) + up_bias.astype(f32)
+    activation, slope = gelu_parts(preact)
+    act_b = activation.astype(bf16)
+    out_part = dot(context, out_weight) + dot(act_b, down_weight)
+    out_sum = lax.psum_scatter(out_part.astype(bf16), "grp", scatter_dimension=0, tiled=True)
+    block_out = inputs[0].astype(f32) + (bias_out + bias_down) + out_sum.astype(f32)
+
+    down_grad = dot(act_b.T, grad_b)
+    out_grad = dot(context.T, grad_b)
+    preact_grad = dot(grad_b, down_weight.T) * slope
+    up_bias_grad = jnp.sum(preact_grad, axis=0)
+    preact_b = preact_grad.astype(bf16)
+    up_grad = dot(mlp_in.T, preact_b)
+    mlp_in_grad = dot(preact_b, w_up.T)
+    context_grad = jnp.transpose(split(dot(grad_b, out_weight.T).astype(bf16)), (1, 0, 2))
+    prob_grad = bdot("hqd,hkd->hqk", context_grad, values)
+    row_dot = jnp.sum(attn_probs * prob_grad, axis=-1, keepdims=True)
+    score_grad = (attn_probs * (prob_grad - row_dot) * scale).astype(bf16)
+    query_grad = bdot("hqk,hkd->qhd", score_grad, keys)
+    key_grad = bdot("hqk,hqd->khd", score_grad, query)
+    value_grad = bdot("hqk,hqd->khd", probs_b, context_grad)
+    qkv_rows = jnp.concatenate(
+        [
+            unrotate(query_grad, cos_table, sin_table).reshape(length, width),
+            unrotate(key_grad, cos_table, sin_table).reshape(length, width),
+            value_grad.reshape(length, width),
+        ],
+        axis=1,
+    )
+    qkv_bias_grad = jnp.sum(qkv_rows, axis=0)
+    qkv_rows_b = qkv_rows.astype(bf16)
+    qkv_grad = dot(attn_in.T, qkv_rows_b)
+    attn_in_grad = dot(qkv_rows_b, w_qkv.T)
+    normed_part = attn_in_grad * gain_attn + mlp_in_grad * gain_mlp
+    normed_grad = lax.psum_scatter(
+        normed_part.astype(bf16), "grp", scatter_dimension=0, tiled=True
+    ).astype(f32)
+    my_normed, my_inverse = layer_norm(inputs[0].astype(f32))
+    input_grad = grad_out + my_inverse * (
+        normed_grad
+        - jnp.mean(normed_grad, axis=-1, keepdims=True)
+        - my_normed * jnp.mean(normed_grad * my_normed, axis=-1, keepdims=True)
+    )
+
+    one_hot = (jnp.arange(group) == me).astype(f32)
+    vectors = jnp.concatenate(
+        [
+            (one_hot[None, :, None] * qkv_bias_grad.reshape(3, 1, width)).reshape(-1),
+            (one_hot[:, None] * up_bias_grad[None]).reshape(-1),
+            jnp.sum(grad_out, axis=0),
+            jnp.sum(attn_in_grad * normed, axis=0),
+            jnp.sum(attn_in_grad, axis=0),
+            jnp.sum(mlp_in_grad * normed, axis=0),
+            jnp.sum(mlp_in_grad, axis=0),
+        ]
+    )
+    vectors = lax.psum(vectors, ("grp", "rep"))
+    nu = up_bias.shape[0]
+    offset = 0
+
+    def take(size):
+        nonlocal offset
+        piece = lax.dynamic_slice_in_dim(vectors, offset + me * size, size)
+        offset += group * size
+        return piece
+
+    qkv_bias_total = take(nb)
+    up_bias_total = take(nu)
+    bias_total, gain_attn_total, shift_attn_total, gain_mlp_total, shift_mlp_total = (
+        take(rows),
+        take(rows),
+        take(rows),
+        take(rows),
+        take(rows),
+    )
+    back = lax.all_to_all(
+        jnp.concatenate([qkv_grad, up_grad], axis=1).astype(bf16).reshape(group, rows, -1),
+        "grp",
+        0,
+        0,
+        tiled=True,
+    )
+    back, rest = lax.psum(
+        (back, jnp.concatenate([down_grad, out_grad], axis=0).astype(bf16)), "rep"
+    )
+    back, rest = back.astype(f32), rest.astype(f32)
+    qkv_total = jnp.transpose(
+        back[:, :, : 3 * width].reshape(group, rows, 3, width), (1, 2, 0, 3)
+    ).reshape(rows, 3 * D)
+    up_total = jnp.transpose(back[:, :, 3 * width :], (1, 0, 2)).reshape(rows, group * hidden)
+    return (
+        block_out[None],
+        input_grad[None],
+        qkv_total,
+        qkv_bias_total,
+        rest[hidden:],
+        bias_total,
+        up_total,
+        up_bias_total,
+        rest[:hidden],
+        bias_total,
+        gain_attn_total,
+        shift_attn_total,
+        gain_mlp_total,
+        shift_mlp_total,
+    )
+
+
 def solution(mesh):
+    local = local_by_tokens if HEADS % mesh.shape["grp"] else local_by_heads
     placed = (
         P("rep", "grp", None),
         P("grp", None),

time: 873 us -> 290 us (0.33)
  waiting for transfers between devices: 610 us -> 60.7 us
  matrix products: 104 us -> 47.8 us
    reduce_scatter x6 -> x2, waiting for transfers between devices: 366 us -> 0.02 us  [the longest x1 0.02 us: local_by_heads(): lax.psum_scatter(out_part.astype(bf16), 'grp', scatter_dimension=0, tiled...]
    all_gather x4 -> x0, waiting for transfers between devices: 144 us -> none  [the longest x1 50.2 us: local(): lax.all_gather(down_weight, 'grp', axis=0, tiled=True)]
    dot_general x96 -> x18, matrix products: 104 us -> 47.8 us  [the longest x12 24.1 us: dot(): return jnp.dot(a, b, preferred_element_type=f32)]
    psum x1, waiting for transfers between devices: 96.8 us -> 51.4 us  [local_by_heads(): lax.psum((back, jnp.concatenate([down_grad, out_grad], axis=0).astype(bf1...]
    psum x1, blocking collectives: 28.2 us -> 41.6 us  [local_by_heads(): vectors = lax.psum(vectors, ('grp', 'rep'))]
    unnamed x79 -> x157, local copies, waits for them, and re-layouts: 20.2 us -> 8.61 us
    reshape x0 -> x6, local copies, waits for them, and re-layouts: none -> 9.77 us  [the longest x2 3.99 us: local_by_heads(): qkv_weight.reshape(rows, 3, group, width)]
    all_to_all x0 -> x2, waiting for transfers between devices: none -> 9.17 us  [the longest x1 9.17 us: local_by_heads(): lax.all_to_all(jnp.concatenate([qkv_grad, up_grad], axis=1).astype(bf16)....]
  transfers between devices with their start and end apart: 11 -> 5, of which waited for: 11 -> 2; matrix products, arithmetic and copies ran while one was open for 6% -> 13% of each run, Pallas kernels for 0% -> 0%
where the time goes in v1:
time: 290 us; the launch traced here: 289 us
  blocking collectives  98.3 us (34%)
  waiting for transfers between devices  60.7 us (21%)
  matrix products  47.8 us (16%)
  local copies, waits for them, and re-layouts  37.7 us (13%)
  other arithmetic  18.6 us (6%)
  between operations  17.1 us (6%)
  starting transfers between devices  9.17 us (3%)
    psum x1, waiting for transfers between devices, local_by_heads(): lax.psum((back, jnp.concatenate([down_grad, out_grad], axis=0).astype(bf1...  51.4 us
    psum x1, blocking collectives, local_by_heads(): vectors = lax.psum(vectors, ('grp', 'rep'))  41.6 us
    unnamed x1, blocking collectives  33.9 us
    dot_general x12, matrix products, dot(): return jnp.dot(a, b, preferred_element_type=f32)  24.1 us
    dot_general x6, matrix products, bdot(): return jnp.einsum(eq, a, b, preferred_element_type=f32)  23.7 us
    all_gather x2, blocking collectives, gather(): return lax.all_gather(array, 'grp', axis=0, tiled=True)  22.8 us
    all_to_all x1, waiting for transfers between devices, local_by_heads(): lax.all_to_all(jnp.concatenate([qkv_grad, up_grad], axis=1).astype(bf16)....  9.17 us
    unnamed x157, local copies, waits for them, and re-layouts  8.61 us
  transfers between devices with their start and end apart: 5, of which 2 were waited for; matrix products, arithmetic and copies ran while one was open for 13% of the time, Pallas kernels for 0%

profile of v1, /device:TPU:0, one launch (start us, length us, event | category | flops | bytes accessed | tf_op | source)
XLA Modules:
  0.0 289.4 jit_solution(12802777104073223455)
XLA Ops:
  8.0 3.0 %reshape.214 = bf16[192,3,4,192]{3,2,1,0:T(4,128)(2,1)S(1)} reshape(bf16[192,2304]{1,0:T(8,128)(2,1)} %param.15) | data formatting | bytes 1769472 | tf_op jit(solution)/shard_map/reshape | solution.py:350
  11.0 1.0 copy.59
  12.7 1.3 copy.76
  14.1 2.1 pad_maximum_fusion
  16.2 5.3 %all-to-all-start = ((bf16[4,192,1344]{2,1,0:T(8,128)(2,1)}), bf16[4,192,1344]{2,1,0:T(8,128)(2,1)}, u32[]{:S(2)}, u32[]{:S(2)}) async-start(bf16[4,192,1344]{2,1,0:T(8,128)(2,1)} %pad_maximum_fusion), calls=%async_computation | async-start | bytes 4325376 | tf_op jit(solution)/shard_map/all_to_all | solution.py:354
  23.3 33.9 %all-reduce = bf16[6912]{0:T(1024)(128)(2,1)S(1)} all-reduce(bf16[6912]{0:T(1024)(128)(2,1)S(1)} %dynamic-update-slice), channel_id=2, replica_groups=mesh['grp'=4,'rep'=8] {'grp'}, use_global_device_ids=true, to_apply=%add | all-reduce | flops 6912 | bytes 27648
  58.0 1.3 fusion.83
  63.9 11.4 %all-gather.1 = bf16[1,512,768]{2,1,0:T(8,128)(2,1)S(1)} all-gather(bf16[1,128,768]{2,1,0:T(8,128)(2,1)S(1)} %copy-done.4), channel_id=3, replica_groups=mesh['grp'=4,'rep'=8] {'grp'}, dimensions={1}, use_global_device_ids=true | all-gather | bytes 983040 | tf_op jit(solution)/shard_map/all_gather | solution.py:316
  75.4 11.4 %all_gather.11 = bf16[512,768]{1,0:T(8,128)(2,1)S(1)} all-gather(bf16[128,768]{1,0:T(8,128)(2,1)} %get-tuple-element.78), channel_id=1, replica_groups=mesh['grp'=4,'rep'=8] {'grp'}, dimensions={0}, use_global_device_ids=true | all-gather | bytes 983040 | tf_op jit(solution)/shard_map/all_gather | solution.py:316
  88.0 1.1 convolution_convert_fusion.5
  89.1 2.1 convolution_add_fusion.1
  91.5 0.8 fusion.4
  92.4 0.7 exponential_reduce_fusion
  93.1 0.9 copy-done.6
  94.6 2.3 fusion.87
  96.9 7.0 %fusion.35 = f32[512,3,64]{0,2,1:T(8,128)S(1)} fusion(f32[3,512,512]{1,2,0:T(8,128)} %fusion.87, bf16[512,3,48]{0,2,1:T(8,128)(2,1)} %copy-done.24, bf16[512,3,8]{0,2,1:T(8,128)(2,1)} %copy-done.32, bf16[512,3,8]{0,2,1:T(8,128)(2,1)} %copy-done.31, f32[3,512,512]{1,2,0:T(8,128)} %copy-done.6, f32[3,512]{1,0:T(4,128)} %log_add_fusion, ...), kind=kOutput, calls=%fused_computation.48 | convolution fusion | flops 109905920 | bytes 7149568 | tf_op jit(solution)/shard_map/hqk,hqd->khd/dot_general | solution.py:392
  103.9 7.8 %fusion.32 = f32[512,3,64]{0,2,1:T(8,128)} fusion(f32[3,512,512]{1,2,0:T(8,128)} %fusion.87, bf16[512,3,48]{0,2,1:T(8,128)(2,1)S(1)} %copy-done.23, bf16[512,3,8]{0,2,1:T(8,128)(2,1)S(1)} %copy-done.28, bf16[512,3,8]{0,2,1:T(8,128)(2,1)S(1)} %copy-done.30, f32[3,512,512]{1,2,0:T(8,128)} %copy-done.6, f32[3,512]{1,0:T(4,128)} %log_add_fusion, ...), kind=kOutput, calls=%fused_computation.47 | convolution fusion | flops 109905920 | bytes 7149568 | tf_op jit(solution)/shard_map/hqk,hkd->qhd/dot_general | solution.py:392
  111.8 0.9 multiply_add_fusion.1
  112.8 2.8 fusion.46
  115.7 3.6 %multiply_convert_fusion.1 = (bf16[512,768]{1,0:T(8,128)(2,1)}, f32[512,768]{1,0:T(8,128)S(1)}) fusion(f32[768]{0:T(1024)S(1)} %copy-done.43, bf16[768,1344]{1,0:T(8,128)(2,1)} %bitcast.6, bf16[1,512,768]{2,1,0:T(8,128)(2,1)S(1)} %all-gather.1, f32[768]{0:T(1024)S(1)} %copy-done.51, f32[768]{0:T(1024)S(1)} %copy-done.48, f32[512]{0:T(512)S(1)} %copy-done.58, ...), kind=kOutput, calls=%fused_computation.36 | convolution fusion | flops 608698368 | bytes 4338688 | tf_op jit(solution)/shard_map/dot_general | solution.py:346
  119.4 1.7 fusion.85
  121.2 2.7 fusion.41
  124.0 4.2 %fusion.80 = (f32[768]{0:T(1024)}, f32[768]{0:T(1024)}, bf16[512,768]{1,0:T(8,128)(2,1)}, f32[768]{0:T(1024)}, f32[768]{0:T(1024)}) fusion(f32[512]{0:T(512)S(1)} %copy-done.58, f32[512]{0:T(512)S(1)} %copy-done.37, bf16[1,512,768]{2,1,0:T(8,128)(2,1)S(1)} %all-gather.1, f32[768]{0:T(1024)S(1)} %copy-done.48, f32[512,768]{1,0:T(8,128)S(1)} %fusion.41, ...), kind=kOutput, calls=%fused_computation.132 | convolution fusion | flops 609088512 | bytes 5134336 | tf_op jit(solution)/shard_map/dot_general | solution.py:346
  128.3 1.8 convolution_convert_fusion.2
  130.1 2.3 copy.66
  132.4 1.0 convolution_convert_fusion.1
  133.6 2.1 pad_maximum_fusion.1
  135.6 3.7 %all-to-all-start.1 = ((bf16[4,192,1344]{2,1,0:T(8,128)(2,1)}), bf16[4,192,1344]{2,1,0:T(8,128)(2,1)S(1)}, u32[]{:S(2)}, u32[]{:S(2)}) async-start(bf16[4,192,1344]{2,1,0:T(8,128)(2,1)} %pad_maximum_fusion.1), calls=%async_computation.3 | async-start | bytes 4325376 | tf_op jit(solution)/shard_map/all_to_all | solution.py:478
  139.4 3.0 %convolution_convert_fusion.4 = bf16[3,64,512]{2,1,0:T(8,128)(2,1)S(1)} fusion(bf16[3,512,64]{1,2,0:T(8,128)(2,1)} %bitcast.163, f32[3,512,512]{1,2,0:T(8,128)} %copy-done.6, f32[3,512]{1,0:T(4,128)S(1)} %copy-done.39, pred[512,512]{0,1:T(8,128)(4,1)} %copy-done.14), kind=kOutput, calls=%fused_computation.51 | convolution fusion | flops 103907328 | bytes 3807232 | tf_op jit(solution)/shard_map/hqk,hkd->qhd/dot_general | solution.py:392
  143.7 1.7 add_convert_fusion.1
  147.1 1.4 fusion.44
  148.5 0.7 mul.506
  149.2 1.6 convolution_convert_fusion.3
  150.8 2.2 convolution_convert_fusion
  153.0 1.2 pad_maximum_fusion.2
  154.3 9.2 %all-to-all-done.1 = bf16[4,192,1344]{2,1,0:T(8,128)(2,1)S(1)} async-done(((bf16[4,192,1344]{2,1,0:T(8,128)(2,1)}), bf16[4,192,1344]{2,1,0:T(8,128)(2,1)S(1)}, u32[]{:S(2)}, u32[]{:S(2)}) %all-to-all-start.1) | async-done | bytes 2064416 | tf_op jit(solution)/shard_map/all_to_all | solution.py:478
  163.4 2.7 copy.67
  167.1 41.6 %psum.22 = f32[9216]{0:T(1024)S(1)} all-reduce(f32[9216]{0:T(1024)S(1)} %constant_dynamic-update-slice_fusion), channel_id=1, replica_groups=mesh['grp'=4,'rep'=8] {'grp','rep'}, use_global_device_ids=true, to_apply=%region_19.20 | all-reduce | flops 9216 | bytes 73728 | tf_op jit(solution)/shard_map/psum | solution.py:459
  210.7 1.1 convert_reduce_fusion.1
  211.9 2.0 fusion.57
  213.9 51.4 %all-reduce.4.cloned.1.call-done = (bf16[4,192,1344]{1,2,0:T(8,128)(2,1)}, bf16[960,768]{1,0:T(8,128)(2,1)}) async-done(((bf16[4,192,1344]{1,2,0:T(8,128)(2,1)}, bf16[960,768]{1,0:T(8,128)(2,1)}), (bf16[4,192,1344]{1,2,0:T(8,128)(2,1)}, bf16[960,768]{1,0:T(8,128)(2,1)})) %all-reduce.4.cloned.1.call-update) | async-done | bytes 3538960 | tf_op jit(solution)/shard_map/psum | solution.py:485
  265.3 1.6 slice.139
  267.5 1.9 slice.141
  269.4 1.6 slice.142
  270.9 0.9 slice.140
  271.8 2.5 copy.68
  274.3 3.7 %reshape.227 = f32[192,2304]{1,0:T(8,128)} reshape(f32[192,3,4,192]{3,2,1,0:T(4,128)} %copy.68) | data formatting | bytes 3538944 | tf_op jit(solution)/shard_map/reshape | solution.py:491
  278.0 3.3 %copy.69 = f32[192,3072]{1,0:T(8,128)} copy(f32[192,3072]{0,1:T(8,128)} %bitcast.143) | data formatting | bytes 4718592
  (213 shorter events, 16.7 us)
Async XLA Ops:
  8.0 111.4 %copy-start = (bf16[768,768]{1,0:T(8,128)(2,1)S(1)}, bf16[768,768]{1,0:T(8,128)(2,1)}, u32[]{:S(2)}) copy-start(bf16[768,768]{1,0:T(8,128)(2,1)} %param.21) | copy-start | bytes 3538948
  16.1 5.5 %copy-start.69 = (u32[32]{0:T(128)S(1)}, u32[32]{0:T(128)}, u32[]{:S(2)}) copy-start(u32[32]{0:T(128)} %constant.79) | copy-start | bytes 388
  16.1 6.8 %copy-start.59 = (bf16[576]{0:T(1024)(128)(2,1)S(1)}, bf16[576]{0:T(1024)(128)(2,1)}, u32[]{:S(2)}) copy-start(bf16[576]{0:T(1024)(128)(2,1)} %param.16) | copy-start | bytes 3460
  16.1 6.8 %copy-start.63 = (bf16[192]{0:T(256)(128)(2,1)S(1)}, bf16[192]{0:T(256)(128)(2,1)}, u32[]{:S(2)}) copy-start(bf16[192]{0:T(256)(128)(2,1)} %param.18) | copy-start | bytes 1156
  16.1 6.8 %copy-start.64 = (bf16[192]{0:T(256)(128)(2,1)S(1)}, bf16[192]{0:T(256)(128)(2,1)}, u32[]{:S(2)}) copy-start(bf16[192]{0:T(256)(128)(2,1)} %param.22) | copy-start | bytes 1156
  16.1 6.8 %copy-start.65 = (bf16[192]{0:T(256)(128)(2,1)S(1)}, bf16[192]{0:T(256)(128)(2,1)}, u32[]{:S(2)}) copy-start(bf16[192]{0:T(256)(128)(2,1)} %param.23) | copy-start | bytes 1156
  16.1 6.8 %copy-start.66 = (bf16[192]{0:T(256)(128)(2,1)S(1)}, bf16[192]{0:T(256)(128)(2,1)}, u32[]{:S(2)}) copy-start(bf16[192]{0:T(256)(128)(2,1)} %param.24) | copy-start | bytes 1156
  16.1 6.8 %copy-start.67 = (bf16[192]{0:T(256)(128)(2,1)S(1)}, bf16[192]{0:T(256)(128)(2,1)}, u32[]{:S(2)}) copy-start(bf16[192]{0:T(256)(128)(2,1)} %param.25) | copy-start | bytes 1156
  16.2 6.8 %copy-start.68 = (bf16[192]{0:T(256)(128)(2,1)S(1)}, bf16[192]{0:T(256)(128)(2,1)}, u32[]{:S(2)}) copy-start(bf16[192]{0:T(256)(128)(2,1)} %param.26) | copy-start | bytes 1156
  16.2 41.8 %copy-start.7 = (f32[1,128,768]{2,1,0:T(8,128)S(1)}, f32[1,128,768]{2,1,0:T(8,128)}, u32[]{:S(2)}) copy-start(f32[1,128,768]{2,1,0:T(8,128)} %param.27) | copy-start | bytes 1179652
  16.2 43.1 %copy-start.4 = (bf16[1,128,768]{2,1,0:T(8,128)(2,1)S(1)}, bf16[1,128,768]{2,1,0:T(8,128)(2,1)}, u32[]{:S(2)}) copy-start(bf16[1,128,768]{2,1,0:T(8,128)(2,1)} %param.14) | copy-start | bytes 589828
  16.2 47.1 %copy-start.55 = (bf16[768]{0:T(1024)(128)(2,1)S(1)}, bf16[768]{0:T(1024)(128)(2,1)}, u32[]{:S(2)}) copy-start(bf16[768]{0:T(1024)(128)(2,1)} %param.20) | copy-start | bytes 4612
  16.2 72.9 %all-to-all-start = ((bf16[4,192,1344]{2,1,0:T(8,128)(2,1)}), bf16[4,192,1344]{2,1,0:T(8,128)(2,1)}, u32[]{:S(2)}, u32[]{:S(2)}) async-start(bf16[4,192,1344]{2,1,0:T(8,128)(2,1)} %pad_maximum_fusion), calls=%async_computation | async-start | bytes 4325376 | tf_op jit(solution)/shard_map/all_to_all | solution.py:354
  21.5 189.1 %reduce-scatter.5.cloned.1.call-start = ((), (), s32[]{:S(2)}) async-start(), calls=%async_computation.5 | async-start | bytes 983040 | tf_op jit(solution)/shard_map/reduce_scatter | solution.py:437
  21.6 70.7 %copy-start.14 = (pred[512,512]{0,1:T(8,128)(4,1)}, pred[512,512]{0,1:T(8,128)(4,1)S(1)}, u32[]{:S(2)}) copy-start(pred[512,512]{0,1:T(8,128)(4,1)S(1)} %iota_compare_fusion) | copy-start | bytes 786436
  61.3 27.8 %copy-start.49 = (f32[768]{0:T(1024)}, f32[768]{0:T(1024)S(1)}, u32[]{:S(2)}) copy-start(f32[768]{0:T(1024)S(1)} %mul.452) | copy-start | bytes 9220
  63.9 23.9 %copy-start.62 = (f32[8]{0:T(128)S(1)}, f32[8]{0:T(128)}, u32[]{:S(2)}) copy-start(f32[8]{0:T(128)} %multiply_power_fusion) | copy-start | bytes 100
  63.9 24.1 %copy-start.11 = (bf16[192,768]{1,0:T(8,128)(2,1)S(1)}, bf16[192,768]{1,0:T(8,128)(2,1)}, u32[]{:S(2)}) copy-start(bf16[192,768]{1,0:T(8,128)(2,1)} %param.17) | copy-start | bytes 884740
  86.7 32.7 %copy-start.2 = (bf16[512,768]{1,0:T(8,128)(2,1)}, bf16[512,768]{1,0:T(8,128)(2,1)S(1)}, u32[]{:S(2)}) copy-start(bf16[512,768]{1,0:T(8,128)(2,1)S(1)} %all_gather.11) | copy-start | bytes 2359300
  86.7 2.4 copy-start.52
  86.9 4.3 %copy-start.36 = (f32[512]{0:T(512)}, f32[512]{0:T(512)S(1)}, u32[]{:S(2)}) copy-start(f32[512]{0:T(512)S(1)} %broadcast_multiply_fusion.2) | copy-start | bytes 6148
  88.0 3.4 %copy-start.25 = (f32[512,8]{0,1:T(8,128)}, f32[512,8]{0,1:T(8,128)S(1)}, u32[]{:S(2)}) copy-start(f32[512,8]{0,1:T(8,128)S(1)} %get-tuple-element.96) | copy-start | bytes 49156
  91.3 3.3 %copy-start.18 = (bf16[512,192]{0,1:T(8,128)(2,1)}, bf16[512,192]{0,1:T(8,128)(2,1)S(1)}, u32[]{:S(2)}) copy-start(bf16[512,192]{0,1:T(8,128)(2,1)S(1)} %slice.172) | copy-start | bytes 589828
  96.9 7.0 %copy-start.23 = (bf16[512,3,48]{0,2,1:T(8,128)(2,1)S(1)}, bf16[512,3,48]{0,2,1:T(8,128)(2,1)}, u32[]{:S(2)}) copy-start(bf16[512,3,48]{0,2,1:T(8,128)(2,1)} %copy-done.22) | copy-start | bytes 442372
  96.9 7.0 %copy-start.28 = (bf16[512,3,8]{0,2,1:T(8,128)(2,1)S(1)}, bf16[512,3,8]{0,2,1:T(8,128)(2,1)}, u32[]{:S(2)}) copy-start(bf16[512,3,8]{0,2,1:T(8,128)(2,1)} %copy-done.27) | copy-start | bytes 73732
  96.9 7.0 %copy-start.30 = (bf16[512,3,8]{0,2,1:T(8,128)(2,1)S(1)}, bf16[512,3,8]{0,2,1:T(8,128)(2,1)}, u32[]{:S(2)}) copy-start(bf16[512,3,8]{0,2,1:T(8,128)(2,1)} %copy-done.29) | copy-start | bytes 73732
  103.9 7.8 %copy-start.13 = (f32[512,3,64]{0,2,1:T(8,128)}, f32[512,3,64]{0,2,1:T(8,128)S(1)}, u32[]{:S(2)}) copy-start(f32[512,3,64]{0,2,1:T(8,128)S(1)} %fusion.35) | copy-start | bytes 1179652
  112.8 2.9 copy-start.37
  112.8 2.9 copy-start.43
  112.8 2.9 copy-start.48
  112.8 2.9 copy-start.51
  112.8 2.9 copy-start.58
  115.7 5.5 %copy-start.20 = (f32[3,64,512]{2,1,0:T(8,128)}, f32[3,64,512]{2,1,0:T(8,128)S(1)}, u32[]{:S(2)}) copy-start(f32[3,64,512]{2,1,0:T(8,128)S(1)} %fusion.46) | copy-start | bytes 1179652
  121.1 2.9 copy-start.71
  121.2 7.1 %copy-start.9 = (f32[512,3,64]{0,2,1:T(8,128)}, f32[512,3,64]{0,2,1:T(8,128)S(1)}, u32[]{:S(2)}) copy-start(f32[512,3,64]{0,2,1:T(8,128)S(1)} %get-tuple-element.103) | copy-start | bytes 1179652
  121.2 7.1 %copy-start.10 = (f32[512,3,64]{0,2,1:T(8,128)}, f32[512,3,64]{0,2,1:T(8,128)S(1)}, u32[]{:S(2)}) copy-start(f32[512,3,64]{0,2,1:T(8,128)S(1)} %get-tuple-element.104) | copy-start | bytes 1179652
  121.2 2.8 copy-start.50
  124.0 4.3 %copy-start.21 = (f32[3,64,512]{2,1,0:T(8,128)S(1)}, f32[3,64,512]{2,1,0:T(8,128)}, u32[]{:S(2)}) copy-start(f32[3,64,512]{2,1,0:T(8,128)} %copy-done.20) | copy-start | bytes 1179652
  124.0 4.3 %copy-start.53 = (f32[768]{0:T(1024)S(1)}, f32[768]{0:T(1024)}, u32[]{:S(2)}) copy-start(f32[768]{0:T(1024)} %add.172) | copy-start | bytes 9220
  135.6 3.8 %copy-start.39 = (f32[3,512]{1,0:T(4,128)S(1)}, f32[3,512]{1,0:T(4,128)}, u32[]{:S(2)}) copy-start(f32[3,512]{1,0:T(4,128)} %log_add_fusion) | copy-start | bytes 18436
  135.6 27.8 %all-to-all-start.1 = ((bf16[4,192,1344]{2,1,0:T(8,128)(2,1)}), bf16[4,192,1344]{2,1,0:T(8,128)(2,1)S(1)}, u32[]{:S(2)}, u32[]{:S(2)}) async-start(bf16[4,192,1344]{2,1,0:T(8,128)(2,1)} %pad_maximum_fusion.1), calls=%async_computation.3 | async-start | bytes 4325376 | tf_op jit(solution)/shard_map/all_to_all | solution.py:478
  139.4 72.5 %reduce-scatter.3.cloned.1.call-start = ((), (), s32[]{:S(2)}) async-start(), calls=%async_computation.4 | async-start | bytes 983040 | tf_op jit(solution)/shard_map/reduce_scatter | solution.py:407
  139.4 3.0 %copy-start.12 = (bf16[192,768]{1,0:T(8,128)(2,1)S(1)}, bf16[192,768]{1,0:T(8,128)(2,1)}, u32[]{:S(2)}) copy-start(bf16[192,768]{1,0:T(8,128)(2,1)} %param.17) | copy-start | bytes 884740
  145.4 119.9 %all-reduce.4.cloned.1.call-start = ((), (), s32[]{:S(2)}) async-start(), calls=%async_computation.6 | async-start | bytes 8454144 | tf_op jit(solution)/shard_map/psum | solution.py:485
  166.1 44.6 %copy-start.41 = (f32[128]{0:T(128)S(1)}, f32[128]{0:T(128)}, u32[]{:S(2)}) copy-start(f32[128]{0:T(128)} %copy-done.40) | copy-start | bytes 1540
  166.1 44.5 %copy-start.60 = (f32[128]{0:T(128)S(1)}, f32[128]{0:T(128)}, u32[]{:S(2)}) copy-start(f32[128]{0:T(128)} %add_rsqrt_fusion.1) | copy-start | bytes 1540
  166.1 45.7 %copy-start.8 = (f32[1,128,768]{2,1,0:T(8,128)S(1)}, f32[1,128,768]{2,1,0:T(8,128)}, u32[]{:S(2)}) copy-start(f32[1,128,768]{2,1,0:T(8,128)} %param.27) | copy-start | bytes 1179652
  209.3 72.0 %copy-start.42 = (f32[192]{0:T(256)}, f32[192]{0:T(256)S(1)}, u32[]{:S(2)}) copy-start(f32[192]{0:T(256)S(1)} %get-tuple-element.130) | copy-start | bytes 2308
  (32 other events, 39.5 us)
Sparse Core Ops, SparseCore 0:
  128.4 37.9 reduce-scatter.4
  169.3 26.3 reduce-scatter.2
Sparse Core Ops, SparseCore 1:
  166.3 99.0 all-reduce.3

commit v2 on v1

--- a/solution.py
+++ b/solution.py
@@ -1,6 +1,10 @@
+import functools
+
 import jax
 import jax.numpy as jnp
 from jax import lax
+from jax.experimental import pallas as pl
+from jax.experimental.pallas import tpu as pltpu
 from jax.sharding import PartitionSpec as P
 
 D = 768
@@ -305,6 +309,238 @@
     )
 
 
+CHUNKS = 4
+
+
+def reduce_kernel(
+    group,
+    stages,
+    grads,
+    vectors,
+    out,
+    vector_out,
+    pair_buf,
+    hop_buf,
+    send_buf,
+    group_buf,
+    total_buf,
+    pair_s,
+    pair_r,
+    hop_s,
+    hop_r,
+    back_s,
+    back_r,
+    last_s,
+    last_r,
+    group_s,
+    group_r,
+    total_s,
+    total_r,
+):
+    f32, bf16 = jnp.float32, jnp.bfloat16
+    members = 2 * stages
+    rep = lax.axis_index("rep")
+    me = lax.axis_index("grp")
+    core = lax.rem(rep, 2)
+    stage = rep // 2
+    partner = stage * 2 + (1 - core)
+
+    barrier = pltpu.get_barrier_semaphore()
+    for i in range(1, members):
+        pl.semaphore_signal(
+            barrier,
+            inc=1,
+            device_id={"rep": lax.rem(rep + i, members)},
+            device_id_type=pl.DeviceIdType.MESH,
+        )
+    for i in range(1, group):
+        pl.semaphore_signal(
+            barrier,
+            inc=1,
+            device_id={"grp": lax.rem(me + i, group)},
+            device_id_type=pl.DeviceIdType.MESH,
+        )
+    pl.semaphore_wait(barrier, members - 1 + group - 1)
+
+    def copy(src, dst, send, recv, where):
+        return pltpu.make_async_remote_copy(
+            src_ref=src,
+            dst_ref=dst,
+            send_sem=send,
+            recv_sem=recv,
+            device_id=where,
+            device_id_type=pl.DeviceIdType.MESH,
+        )
+
+    def place(d):
+        return stage if d == 0 else stages - 1 - stage
+
+    def at(d, step):
+        shift = 2 * step if d == 0 else -2 * step
+        return {"rep": lax.rem(rep + shift + members, members)}
+
+    def pair(d, k):
+        return copy(
+            grads.at[1 - core, d, k],
+            pair_buf.at[d, k],
+            pair_s.at[d, k],
+            pair_r.at[d, k],
+            {"rep": partner},
+        )
+
+    def hop(d, k):
+        return copy(
+            send_buf.at[d, k], hop_buf.at[d, k], hop_s.at[d, k], hop_r.at[d, k], at(d, 1)
+        )
+
+    def back(d, k):
+        return copy(
+            out.at[core, d, k], out.at[core, d, k], back_s.at[d, k], back_r.at[d, k], at(d, -1)
+        )
+
+    def last(d, k, half):
+        return copy(
+            out.at[half, d, k],
+            out.at[half, d, k],
+            last_s.at[d, k],
+            last_r.at[d, k],
+            {"rep": partner},
+        )
+
+    for k in range(CHUNKS):
+        for d in range(2):
+            pair(d, k).start()
+
+    def group_copy(i, slot):
+        peer = lax.rem(me + i, group)
+        return copy(
+            vectors.at[peer], group_buf.at[slot], group_s.at[i - 1], group_r.at[slot], {"grp": peer}
+        )
+
+    def total_copy(i, slot):
+        return copy(
+            total_buf.at[rep],
+            total_buf.at[slot],
+            total_s.at[i - 1],
+            total_r.at[slot],
+            {"rep": lax.rem(rep + i, members)},
+        )
+
+    for i in range(1, group):
+        group_copy(i, me).start()
+    group_buf[me] = vectors[me]
+
+    def reduce_chunk(d, k):
+        position = place(d)
+        pair(d, k).wait_recv()
+        own = grads[core, d, k].astype(f32) + pair_buf[d, k].astype(f32)
+
+        @pl.when(position == 0)
+        def _():
+            send_buf[d, k] = own.astype(bf16)
+            hop(d, k).start()
+
+        @pl.when(position > 0)
+        def _():
+            hop(d, k).wait_recv()
+            total = (own + hop_buf[d, k].astype(f32)).astype(bf16)
+
+            @pl.when(position < stages - 1)
+            def _():
+                send_buf[d, k] = total
+                hop(d, k).start()
+
+            @pl.when(position == stages - 1)
+            def _():
+                out[core, d, k] = total
+                back(d, k).start()
+                last(d, k, core).start()
+
+    def return_chunk(d, k):
+        position = place(d)
+
+        @pl.when(position < stages - 1)
+        def _():
+            back(d, k).wait_recv()
+
+            @pl.when(position > 0)
+            def _():
+                back(d, k).start()
+
+            last(d, k, core).start()
+
+    lag = stages - 1
+    for t in range(CHUNKS + lag):
+        if t < CHUNKS:
+            for d in range(2):
+                reduce_chunk(d, t)
+        if t == 1:
+            for i in range(1, group):
+                group_copy(i, lax.rem(me + group - i, group)).wait_recv()
+            chunk = group_buf[0]
+            for i in range(1, group):
+                chunk = chunk + group_buf[i]
+            total_buf[rep] = chunk
+            for i in range(1, members):
+                total_copy(i, rep).start()
+        if t >= lag:
+            for d in range(2):
+                return_chunk(d, t - lag)
+
+    for i in range(1, members):
+        total_copy(i, lax.rem(rep + members - i, members)).wait_recv()
+    chunk = total_buf[0]
+    for i in range(1, members):
+        chunk = chunk + total_buf[i]
+    vector_out[...] = chunk
+    for i in range(1, group):
+        group_copy(i, me).wait_send()
+    for i in range(1, members):
+        total_copy(i, rep).wait_send()
+    for k in range(CHUNKS):
+        for d in range(2):
+            position = place(d)
+            pair(d, k).wait_send()
+            last(d, k, core).wait_send()
+            last(d, k, 1 - core).wait_recv()
+
+            @pl.when(position < stages - 1)
+            def _():
+                hop(d, k).wait_send()
+
+            @pl.when(position > 0)
+            def _():
+                back(d, k).wait_send()
+
+
+def reduce_over_rep(grads, vectors):
+    group, members = lax.axis_size("grp"), lax.axis_size("rep")
+    tile = grads.shape[3:]
+    chunk = vectors.shape[1:]
+    part = (2, CHUNKS) + tile
+    dma = pltpu.SemaphoreType.DMA
+    vmem = pl.BlockSpec(memory_space=pltpu.VMEM)
+    return pl.pallas_call(
+        functools.partial(reduce_kernel, group, members // 2),
+        out_shape=(
+            jax.ShapeDtypeStruct(grads.shape, grads.dtype),
+            jax.ShapeDtypeStruct(chunk, vectors.dtype),
+        ),
+        in_specs=[vmem, vmem],
+        out_specs=(vmem, vmem),
+        scratch_shapes=[
+            pltpu.VMEM(part, grads.dtype),
+            pltpu.VMEM(part, grads.dtype),
+            pltpu.VMEM(part, grads.dtype),
+            pltpu.VMEM((group,) + chunk, vectors.dtype),
+            pltpu.VMEM((members,) + chunk, vectors.dtype),
+        ]
+        + [dma((2, CHUNKS))] * 8
+        + [dma((group - 1,)), dma((group,)), dma((members - 1,)), dma((members,))],
+        compiler_params=pltpu.CompilerParams(collective_id=0, has_side_effects=True),
+    )(grads, vectors)
+
+
 def rotary_tables(length):
     half_rot = ROT // 2
     frequency = 10000.0 ** (-jnp.arange(half_rot, dtype=jnp.float32) * (2.0 / ROT))
@@ -346,7 +582,15 @@
         return jnp.dot(a, b, preferred_element_type=f32)
 
     grad_out = cotangent[0]
-    x_all, grad_b = (gather(inputs[0]), gather(grad_out.astype(bf16)))
+    small = jnp.concatenate(
+        [qkv_bias, out_bias, down_bias, attn_gain, attn_shift, mlp_gain, mlp_shift]
+    )
+    extra = -(-small.shape[0] // (16 * D)) * 16
+    small = jnp.pad(small, (0, extra * D - small.shape[0])).reshape(extra, D)
+    packed = gather(jnp.concatenate([inputs[0], grad_out.astype(bf16), small], axis=0)[None])
+    x_all = packed[:, :tokens].reshape(length, D)
+    grad_b = packed[:, tokens : 2 * tokens].reshape(length, D)
+    small = packed[:, 2 * tokens :].reshape(group, extra * D).astype(f32)
     qkv_parts = jnp.transpose(qkv_weight.reshape(rows, 3, group, width), (2, 0, 1, 3)).reshape(
         group, rows, 3 * width
     )
@@ -355,11 +599,6 @@
         jnp.concatenate([qkv_parts, up_parts], axis=2), "grp", 0, 0, tiled=True
     ).reshape(D, 3 * width + hidden)
     w_qkv, w_up = w_in[:, : 3 * width], w_in[:, 3 * width :]
-    small = gather(
-        jnp.concatenate(
-            [qkv_bias, out_bias, down_bias, attn_gain, attn_shift, mlp_gain, mlp_shift]
-        )[None]
-    ).astype(f32)
     nb = qkv_bias.shape[0]
     bias_qkv = small[:, :nb].reshape(3, group, width)
     bias_qkv = lax.dynamic_index_in_dim(bias_qkv, me, 1, keepdims=False).reshape(3 * width)
@@ -444,37 +683,25 @@
         - my_normed * jnp.mean(normed_grad * my_normed, axis=-1, keepdims=True)
     )
 
-    one_hot = (jnp.arange(group) == me).astype(f32)
+    mine = jnp.arange(group) == me
+    nb, nu = qkv_bias.shape[0], up_bias.shape[0]
     vectors = jnp.concatenate(
         [
-            (one_hot[None, :, None] * qkv_bias_grad.reshape(3, 1, width)).reshape(-1),
-            (one_hot[:, None] * up_bias_grad[None]).reshape(-1),
-            jnp.sum(grad_out, axis=0),
-            jnp.sum(attn_in_grad * normed, axis=0),
-            jnp.sum(attn_in_grad, axis=0),
-            jnp.sum(mlp_in_grad * normed, axis=0),
-            jnp.sum(mlp_in_grad, axis=0),
-        ]
-    )
-    vectors = lax.psum(vectors, ("grp", "rep"))
-    nu = up_bias.shape[0]
-    offset = 0
-
-    def take(size):
-        nonlocal offset
-        piece = lax.dynamic_slice_in_dim(vectors, offset + me * size, size)
-        offset += group * size
-        return piece
-
-    qkv_bias_total = take(nb)
-    up_bias_total = take(nu)
-    bias_total, gain_attn_total, shift_attn_total, gain_mlp_total, shift_mlp_total = (
-        take(rows),
-        take(rows),
-        take(rows),
-        take(rows),
-        take(rows),
-    )
+            jnp.where(mine[None, :, None], qkv_bias_grad.reshape(3, 1, width), 0.0).reshape(
+                group, nb
+            ),
+            jnp.where(mine[:, None], up_bias_grad[None], 0.0),
+            jnp.sum(grad_out, axis=0).reshape(group, rows),
+            jnp.sum(attn_in_grad * normed, axis=0).reshape(group, rows),
+            jnp.sum(attn_in_grad, axis=0).reshape(group, rows),
+            jnp.sum(mlp_in_grad * normed, axis=0).reshape(group, rows),
+            jnp.sum(mlp_in_grad, axis=0).reshape(group, rows),
+        ],
+        axis=1,
+    )
+    lines = -(-vectors.shape[1] // 1024) * 8
+    vectors = jnp.pad(vectors, ((0, 0), (0, lines * 128 - vectors.shape[1])))
+    vectors = vectors.reshape(group, lines, 128)
     back = lax.all_to_all(
         jnp.concatenate([qkv_grad, up_grad], axis=1).astype(bf16).reshape(group, rows, -1),
         "grp",
@@ -482,10 +709,21 @@
         0,
         tiled=True,
     )
-    back, rest = lax.psum(
-        (back, jnp.concatenate([down_grad, out_grad], axis=0).astype(bf16)), "rep"
-    )
-    back, rest = back.astype(f32), rest.astype(f32)
+    first = back.size // D
+    grads = jnp.concatenate(
+        [back.reshape(first, D), down_grad.astype(bf16), out_grad.astype(bf16)], axis=0
+    )
+    summed, vector_sum = reduce_over_rep(
+        grads.reshape(2, 2, CHUNKS, grads.shape[0] // (4 * CHUNKS), D), vectors
+    )
+    summed = summed.reshape(grads.shape)
+    back, rest = summed[:first].reshape(back.shape).astype(f32), summed[first:].astype(f32)
+    vector_sum = vector_sum.reshape(-1)
+    qkv_bias_total = vector_sum[:nb]
+    up_bias_total = vector_sum[nb : nb + nu]
+    bias_total, gain_attn_total, shift_attn_total, gain_mlp_total, shift_mlp_total = (
+        vector_sum[nb + nu + i * rows : nb + nu + (i + 1) * rows] for i in range(5)
+    )
     qkv_total = jnp.transpose(
         back[:, :, : 3 * width].reshape(group, rows, 3, width), (1, 2, 0, 3)
     ).reshape(rows, 3 * D)
@@ -509,7 +747,9 @@
 
 
 def solution(mesh):
-    local = local_by_tokens if HEADS % mesh.shape["grp"] else local_by_heads
+    group, members = mesh.shape["grp"], mesh.shape["rep"]
+    by_heads = HEADS % group == 0 and members % 2 == 0 and members >= 4
+    local = local_by_heads if by_heads else local_by_tokens
     placed = (
         P("rep", "grp", None),
         P("grp", None),

time: 290 us -> 399 us (1.38)
  Pallas kernels: 0 us -> 190 us
  blocking collectives: 98.3 us -> 0 us
  waiting for transfers between devices: 60.7 us -> 34.7 us
  local copies, waits for them, and re-layouts: 37.7 us -> 62.5 us
  other arithmetic: 18.6 us -> 33.6 us
    pallas_call x0 -> x1, Pallas kernels: none -> 190 us  [reduce_over_rep(): pl.pallas_call(functools.partial(reduce_kernel, group, members // 2), out...]
    psum x1 -> x0, waiting for transfers between devices: 51.4 us -> none  [local_by_heads(): lax.psum((back, jnp.concatenate([down_grad, out_grad], axis=0).astype(bf1...]
    psum x1 -> x0, blocking collectives: 41.6 us -> none  [local_by_heads(): vectors = lax.psum(vectors, ('grp', 'rep'))]
    unnamed x1 -> x0, blocking collectives: 33.9 us -> none
    all_gather x0 -> x1, waiting for transfers between devices: none -> 29.5 us  [gather(): return lax.all_gather(array, 'grp', axis=0, tiled=True)]
    all_gather x2 -> x0, blocking collectives: 22.8 us -> none  [gather(): return lax.all_gather(array, 'grp', axis=0, tiled=True)]
    reshape x0 -> x8, local copies, waits for them, and re-layouts: none -> 11.8 us  [the longest x1 3.98 us: local_by_heads(): back.reshape(first, D)]
    convert_element_type x1, local copies, waits for them, and re-layouts: 0.1 us -> 6.24 us  [local_by_heads(): summed[:first].reshape(back.shape).astype(f32)]
  transfers between devices with their start and end apart: 5 -> 5, of which waited for: 2 -> 2; matrix products, arithmetic and copies ran while one was open for 13% -> 24% of each run, Pallas kernels for 0% -> 48%
where the time goes in v2:
time: 399 us; the launch traced here: 395 us
  Pallas kernels  190 us (48%)
  local copies, waits for them, and re-layouts  62.5 us (16%)
  matrix products  49.7 us (12%)
  waiting for transfers between devices  34.7 us (9%)
  other arithmetic  33.6 us (8%)
  between operations  14.5 us (4%)
  starting transfers between devices  9.9 us (2%)
    pallas_call x1, Pallas kernels, reduce_over_rep(): pl.pallas_call(functools.partial(reduce_kernel, group, members // 2), out...  190 us
    all_gather x1, waiting for transfers between devices, gather(): return lax.all_gather(array, 'grp', axis=0, tiled=True)  29.5 us
    dot_general x12, matrix products, dot(): return jnp.dot(a, b, preferred_element_type=f32)  26.5 us
    dot_general x6, matrix products, bdot(): return jnp.einsum(eq, a, b, preferred_element_type=f32)  23.2 us
    unnamed x91, local copies, waits for them, and re-layouts  8.3 us
  transfers between devices with their start and end apart: 5, of which 2 were waited for; matrix products, arithmetic and copies ran while one was open for 24% of the time, Pallas kernels for 48%

profile of v2, /device:TPU:0, one launch (start us, length us, event | category | flops | bytes accessed | tf_op | source)
XLA Modules:
  0.0 395.2 jit_solution(13248130022432072896)
XLA Ops:
  7.3 4.9 %concatenate.37 = bf16[1728]{0:T(1024)(128)(2,1)S(1)} concatenate(bf16[576]{0:T(1024)(128)(2,1)} %param.16, bf16[192]{0:T(256)(128)(2,1)} %param.18, bf16[192]{0:T(256)(128)(2,1)} %param.22, bf16[192]{0:T(256)(128)(2,1)} %param.23, bf16[192]{0:T(256)(128)(2,1)} %param.24, bf16[192]{0:T(256)(128)(2,1)} %param.25, bf16[192]{0:T(256)(128)(2,1)} %param.26), dimensions={0} | concatenate | bytes 6912 | tf_op jit(solution)/shard_map/concatenate | solution.py:585
  12.2 1.6 fusion.65
  13.9 1.7 pad_maximum_fusion.4
  16.7 2.9 reshape.275
  20.6 1.3 copy.60
  22.0 3.2 pad_maximum_fusion.1
  25.2 5.3 %all-to-all-start = ((bf16[4,192,1344]{2,1,0:T(8,128)(2,1)}), bf16[4,192,1344]{2,1,0:T(8,128)(2,1)}, u32[]{:S(2)}, u32[]{:S(2)}) async-start(bf16[4,192,1344]{2,1,0:T(8,128)(2,1)} %pad_maximum_fusion.1), calls=%async_computation | async-start | bytes 4325376 | tf_op jit(solution)/shard_map/all_to_all | solution.py:598
  35.0 29.5 %all-gather.3.cloned.1.call-done = bf16[1088,768]{1,0:T(8,128)(2,1)} async-done(((bf16[272,768]{1,0:T(8,128)(2,1)}), bf16[1088,768]{1,0:T(8,128)(2,1)}) %all-gather.3.cloned.1.call-update) | async-done | bytes 1671184 | tf_op jit(solution)/shard_map/all_gather | solution.py:552
  72.3 1.5 multiply_reduce_fusion.3
  74.4 1.6 add_convert_fusion.2
  76.1 1.9 convolution_add_fusion.1
  81.4 1.7 fusion.34
  83.1 2.3 fusion.69
  85.4 7.7 %fusion.19 = f32[512,3,64]{0,2,1:T(8,128)} fusion(f32[3,512,512]{1,2,0:T(8,128)} %fusion.69, bf16[512,3,48]{0,2,1:T(8,128)(2,1)} %copy-done.21, bf16[512,3,8]{0,2,1:T(8,128)(2,1)} %copy-done.25, bf16[512,3,8]{0,2,1:T(8,128)(2,1)} %copy-done.26, f32[3,512,512]{1,2,0:T(8,128)} %copy-done.6, f32[3,512]{1,0:T(4,128)} %copy-done.35, ...), kind=kOutput, calls=%fused_computation.41 | convolution fusion | flops 109905920 | bytes 7149568 | tf_op jit(solution)/shard_map/hqk,hkd->qhd/dot_general | solution.py:631
  93.2 7.7 %fusion.22 = f32[512,3,64]{0,2,1:T(8,128)} fusion(f32[3,512,512]{1,2,0:T(8,128)} %fusion.69, bf16[512,3,48]{0,2,1:T(8,128)(2,1)} %copy-done.20, bf16[512,3,8]{0,2,1:T(8,128)(2,1)} %copy-done.24, bf16[512,3,8]{0,2,1:T(8,128)(2,1)} %copy-done.23, f32[3,512,512]{1,2,0:T(8,128)} %copy-done.6, f32[3,512]{1,0:T(4,128)} %copy-done.35, ...), kind=kOutput, calls=%fused_computation.42 | convolution fusion | flops 109905920 | bytes 7149568 | tf_op jit(solution)/shard_map/hqk,hqd->khd/dot_general | solution.py:631
  101.8 3.3 multiply_convert_fusion.1
  105.1 1.7 fusion.67
  107.1 2.3 fusion.28
  109.5 4.4 %multiply_reduce_fusion.1 = (f32[768]{0:T(1024)}, f32[768]{0:T(1024)}, f32[768]{0:T(1024)}, f32[768]{0:T(1024)}, bf16[512,768]{1,0:T(8,128)(2,1)}) fusion(f32[512]{0:T(512)S(1)} %copy-done.34, f32[512]{0:T(512)S(1)} %copy-done.32, bf16[4,272,768]{2,1,0:T(8,128)(2,1)} %bitcast.134, f32[512,768]{1,0:T(8,128)S(1)} %fusion.28, f32[768]{0:T(1024)S(1)} %copy-done.27, ...), kind=kOutput, calls=%fused_computation.23 | convolution fusion | flops 609088512 | bytes 5134336 | tf_op jit(solution)/shard_map/dot_general | solution.py:582
  115.0 3.2 convolution_convert_fusion.1
  118.5 1.9 convolution_convert_fusion.2
  120.5 2.1 pad_maximum_fusion.2
  122.6 4.5 %all-to-all-start.1 = ((bf16[4,192,1344]{2,1,0:T(8,128)(2,1)}), bf16[4,192,1344]{2,1,0:T(8,128)(2,1)S(1)}, u32[]{:S(2)}, u32[]{:S(2)}) async-start(bf16[4,192,1344]{2,1,0:T(8,128)(2,1)} %pad_maximum_fusion.2), calls=%async_computation.3 | async-start | bytes 4325376 | tf_op jit(solution)/shard_map/all_to_all | solution.py:705
  127.1 1.5 fusion.31
  132.1 1.4 reshape.292
  133.4 1.3 reshape.293
  136.9 1.5 concatenate.47
  139.7 2.9 convolution_convert_fusion.4
  143.4 1.8 add_convert_fusion.1
  145.2 2.2 convolution_convert_fusion.3
  147.3 3.2 convolution_convert_fusion
  150.5 5.1 %all-to-all-done.1 = bf16[4,192,1344]{2,1,0:T(8,128)(2,1)S(1)} async-done(((bf16[4,192,1344]{2,1,0:T(8,128)(2,1)}), bf16[4,192,1344]{2,1,0:T(8,128)(2,1)S(1)}, u32[]{:S(2)}, u32[]{:S(2)}) %all-to-all-start.1) | async-done | bytes 2064416 | tf_op jit(solution)/shard_map/all_to_all | solution.py:705
  155.7 4.0 %reshape.288 = bf16[1344,768]{1,0:T(8,128)(2,1)} reshape(bf16[4,192,1344]{2,1,0:T(8,128)(2,1)S(1)} %all-to-all-done.1) | data formatting | bytes 4128768 | tf_op jit(solution)/shard_map/reshape | solution.py:714
  159.7 3.5 pad_maximum_fusion
  163.1 190.4 %shard_map.245 = (bf16[2,2,4,144,768]{4,3,2,1,0:T(8,128)(2,1)}, f32[24,128]{1,0:T(8,128)}) custom-call(bf16[2,2,4,144,768]{4,3,2,1,0:T(8,128)(2,1)} %bitcast.123, f32[4,24,128]{2,1,0:T(8,128)} %bitcast.167), custom_call_target="tpu_custom_call" | custom-call | tf_op jit(solution)/shard_map/pallas_call | solution.py:523
  354.8 1.4 slice.197
  356.1 1.6 slice_convert_fusion.1
  358.6 1.6 slice.198
  361.4 2.3 slice_convert_fusion
  363.7 6.2 %reshape.303 = f32[4,192,1344]{2,1,0:T(8,128)} reshape(f32[1344,768]{1,0:T(8,128)} %slice_convert_fusion) | data formatting | bytes 8257536 | tf_op jit(solution)/shard_map/convert_element_type | solution.py:720
  370.0 1.5 slice-done
  371.5 1.9 copy.67
  373.4 3.0 copy.68
  376.5 2.8 reshape.298
  379.2 2.4 slice_bitcast_fusion
  381.7 1.7 copy.75
  383.4 1.5 fusion.66
  386.2 2.0 fusion.44
  (158 shorter events, 33.9 us)
Async XLA Ops:
  7.2 97.9 %copy-start = (bf16[768,768]{1,0:T(8,128)(2,1)S(1)}, bf16[768,768]{1,0:T(8,128)(2,1)}, u32[]{:S(2)}) copy-start(bf16[768,768]{1,0:T(8,128)(2,1)} %param.21) | copy-start | bytes 3538948
  7.2 8.4 %copy-start.10 = (bf16[192,3072]{1,0:T(8,128)(2,1)S(1)}, bf16[192,3072]{1,0:T(8,128)(2,1)}, u32[]{:S(2)}) copy-start(bf16[192,3072]{1,0:T(8,128)(2,1)} %param.19) | copy-start | bytes 3538948
  7.2 57.3 %all-gather.3.cloned.1.call-start = ((), (), s32[]{:S(2)}) async-start(), calls=%async_computation.6 | async-start | bytes 2088960 | tf_op jit(solution)/shard_map/all_gather | solution.py:552
  20.6 1.4 copy-start.4
  25.2 6.1 %copy-start.2 = (bf16[1,128,768]{2,1,0:T(8,128)(2,1)S(1)}, bf16[1,128,768]{2,1,0:T(8,128)(2,1)}, u32[]{:S(2)}) copy-start(bf16[1,128,768]{2,1,0:T(8,128)(2,1)} %param.14) | copy-start | bytes 589828
  25.2 8.6 %copy-start.39 = (bf16[768]{0:T(1024)(128)(2,1)S(1)}, bf16[768]{0:T(1024)(128)(2,1)}, u32[]{:S(2)}) copy-start(bf16[768]{0:T(1024)(128)(2,1)} %param.20) | copy-start | bytes 4612
  25.2 9.1 %copy-start.29 = (f32[768]{0:T(1024)S(1)}, f32[768]{0:T(1024)}, u32[]{:S(2)}) copy-start(f32[768]{0:T(1024)} %get-tuple-element.51) | copy-start | bytes 9220
  25.2 50.9 %all-to-all-start = ((bf16[4,192,1344]{2,1,0:T(8,128)(2,1)}), bf16[4,192,1344]{2,1,0:T(8,128)(2,1)}, u32[]{:S(2)}, u32[]{:S(2)}) async-start(bf16[4,192,1344]{2,1,0:T(8,128)(2,1)} %pad_maximum_fusion.1), calls=%async_computation | async-start | bytes 4325376 | tf_op jit(solution)/shard_map/all_to_all | solution.py:598
  30.5 354.4 %reduce-scatter.5.cloned.1.call-start = ((), (), s32[]{:S(2)}) async-start(), calls=%async_computation.5 | async-start | bytes 983040 | tf_op jit(solution)/shard_map/reduce_scatter | solution.py:676
  65.7 39.4 %copy-start.1 = (bf16[4,128,768]{2,1,0:T(8,128)(2,1)}, bf16[4,128,768]{2,1,0:T(8,128)(2,1)S(1)}, u32[]{:S(2)}) copy-start(bf16[4,128,768]{2,1,0:T(8,128)(2,1)S(1)} %slice.183) | copy-start | bytes 2359300
  72.3 1.5 copy-start.31
  76.1 2.1 copy-start.22
  78.0 1.0 copy-start.14
  78.1 5.0 %copy-start.15 = (bf16[512,192]{0,1:T(8,128)(2,1)}, bf16[512,192]{0,1:T(8,128)(2,1)S(1)}, u32[]{:S(2)}) copy-start(bf16[512,192]{0,1:T(8,128)(2,1)S(1)} %slice.242) | copy-start | bytes 589828
  78.1 0.7 copy-start.21
  78.2 0.7 copy-start.20
  78.2 1.5 copy-start.23
  78.2 1.5 copy-start.24
  78.2 1.5 copy-start.25
  78.3 1.5 copy-start.26
  79.7 1.6 copy-start.6
  79.7 1.2 copy-start.11
  80.5 2.6 copy-start.35
  105.0 1.7 slice-start.1
  105.1 1.7 slice-start.2
  105.1 2.1 copy-start.19
  106.8 2.7 copy-start.42
  107.1 11.4 %copy-start.8 = (f32[512,3,64]{0,2,1:T(8,128)}, f32[512,3,64]{0,2,1:T(8,128)S(1)}, u32[]{:S(2)}) copy-start(f32[512,3,64]{0,2,1:T(8,128)S(1)} %get-tuple-element.79) | copy-start | bytes 1179652
  107.1 11.4 %copy-start.9 = (f32[512,3,64]{0,2,1:T(8,128)}, f32[512,3,64]{0,2,1:T(8,128)S(1)}, u32[]{:S(2)}) copy-start(f32[512,3,64]{0,2,1:T(8,128)S(1)} %get-tuple-element.80) | copy-start | bytes 1179652
  107.1 2.4 copy-start.27
  107.1 2.4 copy-start.28
  107.1 2.4 copy-start.32
  107.1 2.4 copy-start.34
  118.5 1.9 copy-start.13
  120.4 2.1 copy-start.30
  122.6 17.1 %copy-start.16 = (bf16[512,192]{0,1:T(8,128)(2,1)S(1)}, bf16[512,192]{0,1:T(8,128)(2,1)}, u32[]{:S(2)}) copy-start(bf16[512,192]{0,1:T(8,128)(2,1)} %copy-done.15) | copy-start | bytes 589828
  122.6 33.1 %all-to-all-start.1 = ((bf16[4,192,1344]{2,1,0:T(8,128)(2,1)}), bf16[4,192,1344]{2,1,0:T(8,128)(2,1)S(1)}, u32[]{:S(2)}, u32[]{:S(2)}) async-start(bf16[4,192,1344]{2,1,0:T(8,128)(2,1)} %pad_maximum_fusion.2), calls=%async_computation.3 | async-start | bytes 4325376 | tf_op jit(solution)/shard_map/all_to_all | solution.py:705
  127.1 259.0 %reduce-scatter.3.cloned.1.call-start = ((), (), s32[]{:S(2)}) async-start(), calls=%async_computation.4 | async-start | bytes 983040 | tf_op jit(solution)/shard_map/reduce_scatter | solution.py:646
  139.7 3.0 copy-start.12
  139.7 3.6 copy-start.41
  143.4 1.8 copy-start.18
  358.6 2.9 copy-start.5
  369.9 1.5 slice-start
  381.7 3.2 copy-start.3
  381.7 3.2 copy-start.37
  381.7 3.2 copy-start.40
  381.7 4.4 %copy-start.7 = (f32[1,128,768]{2,1,0:T(8,128)S(1)}, f32[1,128,768]{2,1,0:T(8,128)}, u32[]{:S(2)}) copy-start(f32[1,128,768]{2,1,0:T(8,128)} %param.27) | copy-start | bytes 1179652
  384.9 3.8 copy-start.38
  (3 other events, 1.8 us)
Sparse Core Ops, SparseCore 0:
  15.7 48.7 all-gather.2
  114.0 40.3 reduce-scatter.4
  157.3 28.9 reduce-scatter.2

commit v3 on v1

--- a/solution.py
+++ b/solution.py
@@ -346,7 +346,15 @@
         return jnp.dot(a, b, preferred_element_type=f32)
 
     grad_out = cotangent[0]
-    x_all, grad_b = (gather(inputs[0]), gather(grad_out.astype(bf16)))
+    small = jnp.concatenate(
+        [qkv_bias, out_bias, down_bias, attn_gain, attn_shift, mlp_gain, mlp_shift]
+    )
+    extra = -(-small.shape[0] // (16 * D)) * 16
+    small = jnp.pad(small, (0, extra * D - small.shape[0])).reshape(extra, D)
+    packed = gather(jnp.concatenate([inputs[0], grad_out.astype(bf16), small], axis=0)[None])
+    x_all = packed[:, :tokens].reshape(length, D)
+    grad_b = packed[:, tokens : 2 * tokens].reshape(length, D)
+    small = packed[:, 2 * tokens :].reshape(group, extra * D).astype(f32)
     qkv_parts = jnp.transpose(qkv_weight.reshape(rows, 3, group, width), (2, 0, 1, 3)).reshape(
         group, rows, 3 * width
     )
@@ -355,11 +363,6 @@
         jnp.concatenate([qkv_parts, up_parts], axis=2), "grp", 0, 0, tiled=True
     ).reshape(D, 3 * width + hidden)
     w_qkv, w_up = w_in[:, : 3 * width], w_in[:, 3 * width :]
-    small = gather(
-        jnp.concatenate(
-            [qkv_bias, out_bias, down_bias, attn_gain, attn_shift, mlp_gain, mlp_shift]
-        )[None]
-    ).astype(f32)
     nb = qkv_bias.shape[0]
     bias_qkv = small[:, :nb].reshape(3, group, width)
     bias_qkv = lax.dynamic_index_in_dim(bias_qkv, me, 1, keepdims=False).reshape(3 * width)
@@ -482,9 +485,9 @@
         0,
         tiled=True,
     )
-    back, rest = lax.psum(
-        (back, jnp.concatenate([down_grad, out_grad], axis=0).astype(bf16)), "rep"
-    )
+    rest = lax.psum(jnp.concatenate([down_grad, out_grad], axis=0).astype(bf16), "rep")
+    back, rest = lax.optimization_barrier((back, rest))
+    back = lax.psum(back, "rep")
     back, rest = back.astype(f32), rest.astype(f32)
     qkv_total = jnp.transpose(
         back[:, :, : 3 * width].reshape(group, rows, 3, width), (1, 2, 0, 3)

time: 290 us -> 321 us (1.11)
  waiting for transfers between devices: 60.7 us -> 131 us
  blocking collectives: 98.3 us -> 40.4 us
  local copies, waits for them, and re-layouts: 37.7 us -> 49.7 us
  other arithmetic: 18.6 us -> 28.2 us
    psum x1 -> x2, waiting for transfers between devices: 51.4 us -> 90.9 us  [the longest x1 66.4 us: local_by_heads(): back = lax.psum(back, 'rep')]
    unnamed x1 -> x0, blocking collectives: 33.9 us -> none
    all_gather x0 -> x1, waiting for transfers between devices: none -> 32.4 us  [gather(): return lax.all_gather(array, 'grp', axis=0, tiled=True)]
    all_gather x2 -> x0, blocking collectives: 22.8 us -> none  [gather(): return lax.all_gather(array, 'grp', axis=0, tiled=True)]
    all_to_all x1, waiting for transfers between devices: 9.17 us -> 0.01 us  [local_by_heads(): lax.all_to_all(jnp.concatenate([qkv_grad, up_grad], axis=1).astype(bf16)....]
    reduce_scatter x1, waiting for transfers between devices: 0.02 us -> 7.25 us  [local_by_heads(): lax.psum_scatter(out_part.astype(bf16), 'grp', scatter_dimension=0, tiled...]
    concatenate x1, local copies, waits for them, and re-layouts: 0.09 us -> 4.91 us  [local_by_heads(): jnp.concatenate([qkv_bias, out_bias, down_bias, attn_gain, attn_shift, ml...]
    unnamed x157 -> x125, local copies, waits for them, and re-layouts: 8.61 us -> 12.2 us
  transfers between devices with their start and end apart: 5 -> 7, of which waited for: 2 -> 4; matrix products, arithmetic and copies ran while one was open for 13% -> 20% of each run, Pallas kernels for 0% -> 0%
where the time goes in v3:
time: 321 us; the launch traced here: 319 us
  waiting for transfers between devices  131 us (41%)
  local copies, waits for them, and re-layouts  49.7 us (15%)
  matrix products  45.8 us (14%)
  blocking collectives  40.4 us (13%)
  other arithmetic  28.2 us (9%)
  between operations  14.7 us (5%)
  starting transfers between devices  9.82 us (3%)
    psum x1, waiting for transfers between devices, local_by_heads(): back = lax.psum(back, 'rep')  66.4 us
    psum x1, blocking collectives, local_by_heads(): vectors = lax.psum(vectors, ('grp', 'rep'))  40.4 us
    all_gather x1, waiting for transfers between devices, gather(): return lax.all_gather(array, 'grp', axis=0, tiled=True)  32.4 us
    psum x1, waiting for transfers between devices, local_by_heads(): lax.psum(jnp.concatenate([down_grad, out_grad], axis=0).astype(bf16), 'rep')  24.5 us
    dot_general x12, matrix products, dot(): return jnp.dot(a, b, preferred_element_type=f32)  23.3 us
    dot_general x6, matrix products, bdot(): return jnp.einsum(eq, a, b, preferred_element_type=f32)  22.5 us
    unnamed x125, local copies, waits for them, and re-layouts  12.2 us
    reduce_scatter x1, waiting for transfers between devices, local_by_heads(): lax.psum_scatter(out_part.astype(bf16), 'grp', scatter_dimension=0, tiled...  7.25 us
  transfers between devices with their start and end apart: 7, of which 4 were waited for; matrix products, arithmetic and copies ran while one was open for 20% of the time, Pallas kernels for 0%

profile of v3, /device:TPU:0, one launch (start us, length us, event | category | flops | bytes accessed | tf_op | source)
XLA Modules:
  0.0 319.2 jit_solution(4063550560247214817)
XLA Ops:
  7.3 4.9 %concatenate.38 = bf16[1728]{0:T(1024)(128)(2,1)S(1)} concatenate(bf16[576]{0:T(1024)(128)(2,1)} %param.16, bf16[192]{0:T(256)(128)(2,1)} %param.18, bf16[192]{0:T(256)(128)(2,1)} %param.22, bf16[192]{0:T(256)(128)(2,1)} %param.23, bf16[192]{0:T(256)(128)(2,1)} %param.24, bf16[192]{0:T(256)(128)(2,1)} %param.25, bf16[192]{0:T(256)(128)(2,1)} %param.26), dimensions={0} | concatenate | bytes 6912 | tf_op jit(solution)/shard_map/concatenate | solution.py:349
  12.2 1.6 fusion.65
  13.9 1.7 pad_maximum_fusion.4
  16.7 2.9 reshape.247
  20.6 1.3 copy.49
  22.0 3.2 %pad_maximum_fusion = bf16[4,192,1344]{2,1,0:T(8,128)(2,1)} fusion(bf16[4,192,768]{2,1,0:T(8,128)(2,1)S(1)} %bitcast.128, bf16[4,192,576]{2,1,0:T(8,128)(2,1)} %copy.49), kind=kLoop, calls=%fused_computation.10 | loop fusion | flops 4128768 | bytes 4128768 | tf_op jit(solution)/shard_map/concatenate | solution.py:363
  25.2 5.3 %all-to-all-start = ((bf16[4,192,1344]{2,1,0:T(8,128)(2,1)}), bf16[4,192,1344]{2,1,0:T(8,128)(2,1)}, u32[]{:S(2)}, u32[]{:S(2)}) async-start(bf16[4,192,1344]{2,1,0:T(8,128)(2,1)} %pad_maximum_fusion), calls=%async_computation | async-start | bytes 4325376 | tf_op jit(solution)/shard_map/all_to_all | solution.py:362
  32.1 32.4 %all-gather.3.cloned.1.call-done = bf16[1088,768]{1,0:T(8,128)(2,1)} async-done(((bf16[272,768]{1,0:T(8,128)(2,1)}), bf16[1088,768]{1,0:T(8,128)(2,1)}) %all-gather.3.cloned.1.call-update) | async-done | bytes 1671184 | tf_op jit(solution)/shard_map/all_gather | solution.py:316
  67.9 1.3 convert_reduce_fusion
  69.2 1.5 multiply_reduce_fusion.3
  70.7 2.5 add_convert_fusion.2
  73.3 1.9 convolution_add_fusion.1
  77.9 1.7 fusion.34
  79.7 2.3 fusion.69
  82.0 6.9 %fusion.19 = f32[512,3,64]{0,2,1:T(8,128)S(1)} fusion(f32[3,512,512]{1,2,0:T(8,128)} %fusion.69, bf16[512,3,48]{0,2,1:T(8,128)(2,1)S(1)} %copy-done.26, bf16[512,3,8]{0,2,1:T(8,128)(2,1)S(1)} %copy-done.31, bf16[512,3,8]{0,2,1:T(8,128)(2,1)S(1)} %copy-done.33, f32[3,512,512]{1,2,0:T(8,128)} %copy-done.5, f32[3,512]{1,0:T(4,128)} %copy-done.44, ...), kind=kOutput, calls=%fused_computation.39 | convolution fusion | flops 109905920 | bytes 7149568 | tf_op jit(solution)/shard_map/hqk,hkd->qhd/dot_general | solution.py:395
  88.9 7.9 %fusion.22 = f32[512,3,64]{0,2,1:T(8,128)} fusion(f32[3,512,512]{1,2,0:T(8,128)} %fusion.69, bf16[512,3,48]{0,2,1:T(8,128)(2,1)} %copy-done.24, bf16[512,3,8]{0,2,1:T(8,128)(2,1)} %copy-done.29, bf16[512,3,8]{0,2,1:T(8,128)(2,1)} %copy-done.28, f32[3,512,512]{1,2,0:T(8,128)} %copy-done.5, f32[3,512]{1,0:T(4,128)} %copy-done.44, pred[512,512]{0,1:T(8,128)(4,1)} %copy-done.14), kind=kOutput, calls=%fused_computation.40 | convolution fusion | flops 109905920 | bytes 7149568 | tf_op jit(solution)/shard_map/hqk,hqd->khd/dot_general | solution.py:395
  96.8 1.5 multiply_add_fusion.1
  98.4 2.9 convolution_convert_fusion.4
  101.6 3.5 %multiply_convert_fusion.1 = (bf16[512,768]{1,0:T(8,128)(2,1)S(1)}, f32[512,768]{1,0:T(8,128)}) fusion(f32[768]{0:T(1024)S(1)} %copy-done.48, bf16[512,768]{1,0:T(8,128)(2,1)S(1)} %copy-done.6, bf16[768,1344]{1,0:T(8,128)(2,1)} %bitcast.9), kind=kOutput, calls=%fused_computation.25 | convolution fusion | flops 606339072 | bytes 4328448 | tf_op jit(solution)/shard_map/dot_general | solution.py:346
  108.4 3.1 fusion.67
  111.8 2.5 fusion.28
  114.3 4.5 %multiply_reduce_fusion.1 = (f32[768]{0:T(1024)}, f32[768]{0:T(1024)}, f32[768]{0:T(1024)}, f32[768]{0:T(1024)}, bf16[512,768]{1,0:T(8,128)(2,1)}) fusion(f32[512]{0:T(512)S(1)} %copy-done.43, f32[512]{0:T(512)S(1)} %copy-done.41, bf16[4,272,768]{2,1,0:T(8,128)(2,1)} %bitcast.125, f32[512,768]{1,0:T(8,128)S(1)} %fusion.28, f32[768]{0:T(1024)S(1)} %copy-done.36, ...), kind=kOutput, calls=%fused_computation.21 | convolution fusion | flops 609088512 | bytes 5134336 | tf_op jit(solution)/shard_map/dot_general | solution.py:346
  120.4 2.0 convolution_convert_fusion.2
  123.2 2.1 pad_maximum_fusion.1
  125.3 4.4 %all-to-all-start.1 = ((bf16[4,192,1344]{2,1,0:T(8,128)(2,1)}), bf16[4,192,1344]{2,1,0:T(8,128)(2,1)S(1)}, u32[]{:S(2)}, u32[]{:S(2)}) async-start(bf16[4,192,1344]{2,1,0:T(8,128)(2,1)} %pad_maximum_fusion.1), calls=%async_computation.3 | async-start | bytes 4325376 | tf_op jit(solution)/shard_map/all_to_all | solution.py:481
  129.7 1.5 fusion.68
  131.2 1.7 add_convert_fusion.1
  133.7 1.4 fusion.31
  136.7 1.3 broadcast_multiply_fusion
  138.1 1.3 mul.514
  139.4 1.3 constant_dynamic-update-slice_fusion.6
  140.7 1.4 constant_dynamic-update-slice_fusion.5
  143.4 1.3 constant_dynamic-update-slice_fusion.3
  144.7 1.3 constant_dynamic-update-slice_fusion.2
  146.0 1.3 constant_dynamic-update-slice_fusion.1
  147.3 24.5 %all-reduce.4.cloned.1.call-done = bf16[960,768]{1,0:T(8,128)(2,1)} async-done(((bf16[960,768]{1,0:T(8,128)(2,1)}), bf16[960,768]{1,0:T(8,128)(2,1)}) %all-reduce.4.cloned.1.call-update) | async-done | bytes 1474576 | tf_op jit(solution)/shard_map/psum | solution.py:488
  171.8 1.3 copy-done.1
  174.5 40.4 %psum.23 = f32[9216]{0:T(1024)S(1)} all-reduce(f32[9216]{0:T(1024)} %constant_dynamic-update-slice_fusion), channel_id=1, replica_groups=mesh['grp'=4,'rep'=8] {'grp','rep'}, use_global_device_ids=true, to_apply=%region_20.21 | all-reduce | flops 9216 | bytes 73728 | tf_op jit(solution)/shard_map/psum | solution.py:462
  216.9 1.8 slice.155
  218.7 2.9 slice.157
  222.8 7.3 %reduce-scatter.3.cloned.1.call-done = bf16[128,768]{1,0:T(8,128)(2,1)} async-done(((bf16[512,768]{1,0:T(8,128)(2,1)}), bf16[128,768]{1,0:T(8,128)(2,1)}) %reduce-scatter.3.cloned.1.call-update) | async-done | bytes 196624 | tf_op jit(solution)/shard_map/reduce_scatter | solution.py:410
  230.1 2.0 fusion.44
  232.1 66.4 %all-reduce.6.cloned.1.call-done = bf16[4,192,1344]{2,1,0:T(8,128)(2,1)} async-done(((bf16[4,192,1344]{2,1,0:T(8,128)(2,1)}), bf16[4,192,1344]{2,1,0:T(8,128)(2,1)}) %all-reduce.6.cloned.1.call-update) | async-done | bytes 2064400 | tf_op jit(solution)/shard_map/psum | solution.py:490
  298.4 2.6 slice.154
  301.0 2.0 copy.56
  303.0 2.5 copy.57
  305.6 3.8 %reshape.261 = f32[192,2304]{1,0:T(8,128)} reshape(f32[192,3,4,192]{3,2,1,0:T(4,128)} %copy.57) | data formatting | bytes 3538944 | tf_op jit(solution)/shard_map/reshape | solution.py:494
  310.4 1.7 copy.64
  (191 shorter events, 25.4 us)
Async XLA Ops:
  7.2 101.2 %copy-start = (bf16[768,768]{1,0:T(8,128)(2,1)S(1)}, bf16[768,768]{1,0:T(8,128)(2,1)}, u32[]{:S(2)}) copy-start(bf16[768,768]{1,0:T(8,128)(2,1)} %param.21) | copy-start | bytes 3538948
  7.2 8.4 %copy-start.11 = (bf16[192,3072]{1,0:T(8,128)(2,1)S(1)}, bf16[192,3072]{1,0:T(8,128)(2,1)}, u32[]{:S(2)}) copy-start(bf16[192,3072]{1,0:T(8,128)(2,1)} %param.19) | copy-start | bytes 3538948
  7.2 57.3 %all-gather.3.cloned.1.call-start = ((), (), s32[]{:S(2)}) async-start(), calls=%async_computation.8 | async-start | bytes 2088960 | tf_op jit(solution)/shard_map/all_gather | solution.py:316
  25.2 5.3 %copy-start.3 = (bf16[1,128,768]{2,1,0:T(8,128)(2,1)S(1)}, bf16[1,128,768]{2,1,0:T(8,128)(2,1)}, u32[]{:S(2)}) copy-start(bf16[1,128,768]{2,1,0:T(8,128)(2,1)} %param.14) | copy-start | bytes 589828
  25.2 6.2 %copy-start.50 = (bf16[768]{0:T(1024)(128)(2,1)S(1)}, bf16[768]{0:T(1024)(128)(2,1)}, u32[]{:S(2)}) copy-start(bf16[768]{0:T(1024)(128)(2,1)} %param.20) | copy-start | bytes 4612
  25.2 48.1 %all-to-all-start = ((bf16[4,192,1344]{2,1,0:T(8,128)(2,1)}), bf16[4,192,1344]{2,1,0:T(8,128)(2,1)}, u32[]{:S(2)}, u32[]{:S(2)}) async-start(bf16[4,192,1344]{2,1,0:T(8,128)(2,1)} %pad_maximum_fusion), calls=%async_computation | async-start | bytes 4325376 | tf_op jit(solution)/shard_map/all_to_all | solution.py:362
  30.5 141.3 %all-reduce.4.cloned.1.call-start = ((), (), s32[]{:S(2)}) async-start(), calls=%async_computation.6 | async-start | bytes 2949120 | tf_op jit(solution)/shard_map/psum | solution.py:488
  31.3 44.1 %copy-start.27 = (f32[512,8]{0,1:T(8,128)}, f32[512,8]{0,1:T(8,128)S(1)}, u32[]{:S(2)}) copy-start(f32[512,8]{0,1:T(8,128)S(1)} %get-tuple-element.58) | copy-start | bytes 49156
  31.4 46.5 %copy-start.14 = (pred[512,512]{0,1:T(8,128)(4,1)}, pred[512,512]{0,1:T(8,128)(4,1)S(1)}, u32[]{:S(2)}) copy-start(pred[512,512]{0,1:T(8,128)(4,1)S(1)} %iota_compare_fusion) | copy-start | bytes 786436
  67.5 5.7 %copy-start.35 = (f32[768]{0:T(1024)}, f32[768]{0:T(1024)S(1)}, u32[]{:S(2)}) copy-start(f32[768]{0:T(1024)S(1)} %mul.471) | copy-start | bytes 9220
  67.7 5.6 %copy-start.37 = (f32[768]{0:T(1024)}, f32[768]{0:T(1024)S(1)}, u32[]{:S(2)}) copy-start(f32[768]{0:T(1024)S(1)} %mul.453) | copy-start | bytes 9220
  69.2 5.9 %copy-start.40 = (f32[512]{0:T(512)}, f32[512]{0:T(512)S(1)}, u32[]{:S(2)}) copy-start(f32[512]{0:T(512)S(1)} %get-tuple-element.55) | copy-start | bytes 6148
  70.7 4.4 %copy-start.42 = (f32[512]{0:T(512)}, f32[512]{0:T(512)S(1)}, u32[]{:S(2)}) copy-start(f32[512]{0:T(512)S(1)} %rsqrt_bitcast_fusion) | copy-start | bytes 6148
  75.3 4.4 %copy-start.15 = (bf16[512,192]{0,1:T(8,128)(2,1)}, bf16[512,192]{0,1:T(8,128)(2,1)S(1)}, u32[]{:S(2)}) copy-start(bf16[512,192]{0,1:T(8,128)(2,1)S(1)} %slice.195) | copy-start | bytes 589828
  77.0 2.6 copy-start.44
  88.9 7.9 %copy-start.13 = (f32[512,3,64]{0,2,1:T(8,128)}, f32[512,3,64]{0,2,1:T(8,128)S(1)}, u32[]{:S(2)}) copy-start(f32[512,3,64]{0,2,1:T(8,128)S(1)} %fusion.19) | copy-start | bytes 1179652
  88.9 9.4 %copy-start.16 = (bf16[512,192]{0,1:T(8,128)(2,1)S(1)}, bf16[512,192]{0,1:T(8,128)(2,1)}, u32[]{:S(2)}) copy-start(bf16[512,192]{0,1:T(8,128)(2,1)} %copy-done.15) | copy-start | bytes 589828
  98.3 3.3 %copy-start.6 = (bf16[512,768]{1,0:T(8,128)(2,1)S(1)}, bf16[512,768]{1,0:T(8,128)(2,1)}, u32[]{:S(2)}) copy-start(bf16[512,768]{1,0:T(8,128)(2,1)} %get-tuple-element.25) | copy-start | bytes 2359300
  98.3 3.3 %copy-start.48 = (f32[768]{0:T(1024)S(1)}, f32[768]{0:T(1024)}, u32[]{:S(2)}) copy-start(f32[768]{0:T(1024)} %convert_element_type.109) | copy-start | bytes 9220
  101.3 3.9 %copy-start.18 = (bf16[3,64,512]{2,1,0:T(8,128)(2,1)}, bf16[3,64,512]{2,1,0:T(8,128)(2,1)S(1)}, u32[]{:S(2)}) copy-start(bf16[3,64,512]{2,1,0:T(8,128)(2,1)S(1)} %convolution_convert_fusion.4) | copy-start | bytes 589828
  108.3 113.3 %reduce-scatter.5.cloned.1.call-start = ((), (), s32[]{:S(2)}) async-start(), calls=%async_computation.5 | async-start | bytes 983040 | tf_op jit(solution)/shard_map/reduce_scatter | solution.py:440
  108.4 3.2 %slice-start = ((f32[512,3,64]{0,2,1:T(8,128)}), f32[512,3,48]{0,2,1:T(8,128)S(1)}, s32[]{:S(2)}) async-start(f32[512,3,64]{0,2,1:T(8,128)} %copy-done.13), calls=%async_computation.9 | async-start | bytes 589824 | tf_op jit(solution)/shard_map/slice | solution.py:57
  108.4 3.2 %slice-start.1 = ((f32[512,3,64]{0,2,1:T(8,128)}), f32[512,3,48]{0,2,1:T(8,128)S(1)}, s32[]{:S(2)}) async-start(f32[512,3,64]{0,2,1:T(8,128)} %fusion.22), calls=%async_computation.10 | async-start | bytes 589824 | tf_op jit(solution)/shard_map/slice | solution.py:57
  108.4 3.2 %copy-start.20 = (f32[512,3,8]{0,2,1:T(8,128)S(1)}, f32[512,3,8]{0,2,1:T(8,128)}, u32[]{:S(2)}) copy-start(f32[512,3,8]{0,2,1:T(8,128)} %get-tuple-element.29) | copy-start | bytes 147460
  108.4 3.2 %copy-start.21 = (f32[512,3,8]{0,2,1:T(8,128)S(1)}, f32[512,3,8]{0,2,1:T(8,128)}, u32[]{:S(2)}) copy-start(f32[512,3,8]{0,2,1:T(8,128)} %get-tuple-element.30) | copy-start | bytes 147460
  108.4 3.2 %copy-start.22 = (f32[512,3,8]{0,2,1:T(8,128)S(1)}, f32[512,3,8]{0,2,1:T(8,128)}, u32[]{:S(2)}) copy-start(f32[512,3,8]{0,2,1:T(8,128)} %get-tuple-element.51) | copy-start | bytes 147460
  108.4 3.2 %copy-start.23 = (f32[512,3,8]{0,2,1:T(8,128)S(1)}, f32[512,3,8]{0,2,1:T(8,128)}, u32[]{:S(2)}) copy-start(f32[512,3,8]{0,2,1:T(8,128)} %get-tuple-element.52) | copy-start | bytes 147460
  108.4 3.3 %copy-start.19 = (f32[3,64,512]{2,1,0:T(8,128)S(1)}, f32[3,64,512]{2,1,0:T(8,128)}, u32[]{:S(2)}) copy-start(f32[3,64,512]{2,1,0:T(8,128)} %fusion.34) | copy-start | bytes 1179652
  111.6 2.7 copy-start.56
  111.7 2.5 copy-start.10
  111.7 8.6 %copy-start.9 = (f32[512,3,64]{0,2,1:T(8,128)}, f32[512,3,64]{0,2,1:T(8,128)S(1)}, u32[]{:S(2)}) copy-start(f32[512,3,64]{0,2,1:T(8,128)S(1)} %get-tuple-element.65) | copy-start | bytes 1179652
  111.7 2.5 copy-start.36
  111.8 2.5 copy-start.38
  111.8 2.5 copy-start.41
  114.3 4.5 %copy-start.53 = (f32[128]{0:T(128)S(1)}, f32[128]{0:T(128)}, u32[]{:S(2)}) copy-start(f32[128]{0:T(128)} %convert_reduce_fusion.2) | copy-start | bytes 1540
  114.3 4.6 %copy-start.7 = (bf16[512,768]{1,0:T(8,128)(2,1)S(1)}, bf16[512,768]{1,0:T(8,128)(2,1)}, u32[]{:S(2)}) copy-start(bf16[512,768]{1,0:T(8,128)(2,1)} %get-tuple-element.25) | copy-start | bytes 2359300
  118.9 14.1 %copy-start.45 = (f32[128]{0:T(128)}, f32[128]{0:T(128)S(1)}, u32[]{:S(2)}) copy-start(f32[128]{0:T(128)S(1)} %broadcast_multiply_fusion.5) | copy-start | bytes 1540
  125.3 46.5 %all-to-all-start.1 = ((bf16[4,192,1344]{2,1,0:T(8,128)(2,1)}), bf16[4,192,1344]{2,1,0:T(8,128)(2,1)S(1)}, u32[]{:S(2)}, u32[]{:S(2)}) async-start(bf16[4,192,1344]{2,1,0:T(8,128)(2,1)} %pad_maximum_fusion.1), calls=%async_computation.3 | async-start | bytes 4325376 | tf_op jit(solution)/shard_map/all_to_all | solution.py:481
  129.7 100.4 %reduce-scatter.3.cloned.1.call-start = ((), (), s32[]{:S(2)}) async-start(), calls=%async_computation.4 | async-start | bytes 983040 | tf_op jit(solution)/shard_map/reduce_scatter | solution.py:410
  132.9 9.2 %copy-start.34 = (f32[768]{0:T(1024)S(1)}, f32[768]{0:T(1024)}, u32[]{:S(2)}) copy-start(f32[768]{0:T(1024)} %get-tuple-element.37) | copy-start | bytes 9220
  132.9 165.5 %all-reduce.6.cloned.1.call-start = ((), (), s32[]{:S(2)}) async-start(), calls=%async_computation.7 | async-start | bytes 4325376 | tf_op jit(solution)/shard_map/psum | solution.py:490
  140.7 32.5 %copy-start.49 = (f32[768]{0:T(1024)S(1)}, f32[768]{0:T(1024)}, u32[]{:S(2)}) copy-start(f32[768]{0:T(1024)} %get-tuple-element.21) | copy-start | bytes 9220
  140.7 33.7 %copy-start.39 = (f32[4,192]{1,0:T(4,128)S(1)}, f32[4,192]{1,0:T(4,128)}, u32[]{:S(2)}) copy-start(f32[4,192]{1,0:T(4,128)} %get-tuple-element.41) | copy-start | bytes 9220
  216.9 95.1 %copy-start.47 = (f32[192]{0:T(256)}, f32[192]{0:T(256)S(1)}, u32[]{:S(2)}) copy-start(f32[192]{0:T(256)S(1)} %get-tuple-element.92) | copy-start | bytes 2308
  218.7 2.9 copy-start.46
  218.7 2.9 copy-start.52
  218.7 11.3 %copy-start.8 = (f32[1,128,768]{2,1,0:T(8,128)S(1)}, f32[1,128,768]{2,1,0:T(8,128)}, u32[]{:S(2)}) copy-start(f32[1,128,768]{2,1,0:T(8,128)} %param.27) | copy-start | bytes 1179652
  305.6 3.8 %copy-start.2 = (bf16[4,192,1344]{2,1,0:T(8,128)(2,1)S(1)}, bf16[4,192,1344]{2,1,0:T(8,128)(2,1)}, u32[]{:S(2)}) copy-start(bf16[4,192,1344]{2,1,0:T(8,128)(2,1)} %all-reduce.6.cloned.1.call-done) | copy-start | bytes 6193156
  (19 other events, 29.0 us)
Sparse Core Ops, SparseCore 0:
  15.7 48.7 all-gather.2
  108.4 63.3 all-reduce.3
  175.3 25.8 reduce-scatter.4
  203.9 26.1 reduce-scatter.2
  232.9 65.4 all-reduce.5
